TPU v7x, 128 devices: a whole 4x4x4 slice. The times are simulated.
128 devices in a mesh: bond: 16 (over x, z), sector: 8 (over y, core).
Axes of the slice: x: 4, y: 4, z: 4, core: 2. Of those that a mesh axis runs over, the one named last changes fastest.
Arguments:
- theta: bfloat16 [8, 768, 768], P('sector'), may hold values from -80 to 80
- sector_dims: int32 [8], P('sector'), may hold values from 1 to 768, 4608 in all
- right_dims: int32 [8], P('sector'), may hold values from 1 to 768, 4608 in all
- env_left: bfloat16 [32, 8, 768, 768], P('bond', 'sector'), may hold values from -0.21875 to 0.21875
- env_right: bfloat16 [32, 8, 768, 768], P('bond', 'sector'), may hold values from -0.21875 to 0.21875
- mpo_on: int32 [32], P('bond'), may hold values 0 or 1
- mpo_coef: float32 [32], P('bond'), may hold values from -3 to 3
- mix_index: int32 [32, 3], P('bond'), may hold values from 0 to 7
- weight_table: float32 [8], replicated, may hold values from -3 to 3
Outputs:
- matvec: bfloat16 [8, 768, 768], P('sector', 'bond')
- env_next: bfloat16 [32, 8, 768, 768], P('bond', 'sector')
All inputs are finite; a program needn't handle non-finite values. No bound on the sum of `sector_dims` or of `right_dims` or of `mpo_on` on one device may be relied on, other than what follows from the above.
Results may differ from a plain program's by a relative error of at most 0.008.
Values may be sent and summed in bfloat16 or wider, within the bound.
A program may use at most 64 MiB of HBM per device.

v0:
```python
import math

import jax
import jax.numpy as jnp
from jax import lax
from jax.sharding import Mesh
from jax.sharding import PartitionSpec as P

BOND = ("bond_0", "bond_1")
SECTOR = ("sector_0", "sector_1")
BOND_SECTOR = ("bond_0", "bond_1", "sector_0", "sector_1")


def padded(shard, sides, width):
    for axis, dim in sides:
        peers, length = (lax.axis_size(axis), shard.shape[dim])
        up = [(i, (i + 1) % peers) for i in range(peers - 1)]
        down = [(j, i) for i, j in up]
        last = lax.slice_in_dim(shard, length - width, length, axis=dim)
        first = lax.slice_in_dim(shard, 0, width, axis=dim)
        before = lax.ppermute(last, axis, up)
        after = lax.ppermute(first, axis, down)
        shard = jnp.concatenate([before, shard, after], axis=dim)
    return shard


def in_blocks(shard, dim, peers):
    dims = shard.shape
    parts = shard.reshape(*dims[:dim], peers, dims[dim] // peers, *dims[dim + 1 :])
    return jnp.moveaxis(parts, dim, 0)


def sum_at_owner(shard, axis, dim):
    parts = in_blocks(shard, dim, lax.axis_size(axis))
    arrived = lax.all_to_all(parts, axis, split_axis=0, concat_axis=0, tiled=True)
    return arrived.sum(axis=0)


def one_axis_at_a_time(shard, axes):
    for axis in axes:
        shard = lax.psum(shard, axis)
    return shard


def laid_out(parts, dim):
    dims = list(parts.shape[1:])
    dims[dim] *= parts.shape[0]
    return jnp.moveaxis(parts, 0, dim).reshape(dims)


def copy_for_each(shard, axis):
    copies = jnp.broadcast_to(shard, (lax.axis_size(axis), *shard.shape))
    return lax.all_to_all(copies, axis, split_axis=0, concat_axis=0, tiled=True)


def collect(shard, axis, dim):
    return laid_out(copy_for_each(shard, axis), dim)


def on_device(
    theta, sector_dims, right_dims, env_left, env_right, mpo_on, mpo_coef, mix_index, weight_table
):
    states = theta.shape[1]
    bond_local = env_left.shape[0]
    index = jnp.arange(states, dtype=jnp.int32)
    row_flag = index < sector_dims[0]
    col_flag = index < right_dims[0]
    row_live = row_flag.astype(jnp.float32)
    col_live = col_flag.astype(jnp.float32)
    live = jnp.where(row_flag[:, None] & col_flag[None, :], theta[0], jnp.zeros_like(theta[0]))
    gain = mpo_coef * mpo_on.astype(jnp.float32)
    rims = padded(env_left, ((BOND, 0),), 1)
    share = states // lax.axis_size(BOND)
    first = lax.axis_index(BOND) * share
    count_all = lax.axis_size(SECTOR) * states * states
    total = jnp.zeros((share * lax.axis_size(BOND), states), jnp.float32)
    for term_channel in range(bond_local):
        block = env_left[term_channel, 0]
        applied = jnp.dot(block, live, preferred_element_type=jnp.float32).astype(jnp.bfloat16)
        total = total + gain[term_channel] * lax.dot_general(
            applied,
            env_right[term_channel, 0],
            (((1,), (1,)), ((), ())),
            preferred_element_type=jnp.float32,
        )
    rows_sum = sum_at_owner(total, BOND, 0)
    row_part = lax.dynamic_slice_in_dim(row_live, first, share, 0)
    product_rows = rows_sum * row_part[:, None] * col_live[None, :]
    square_total = one_axis_at_a_time(jnp.sum(product_rows * product_rows), BOND_SECTOR)
    scale = lax.rsqrt(square_total / count_all + 1e-06)
    unit_part = (product_rows * scale).astype(jnp.bfloat16)
    unit = collect(unit_part, BOND, 0)
    matvec = product_rows.astype(jnp.bfloat16)[None]
    table_index = jnp.arange(weight_table.shape[0], dtype=jnp.int32)
    mix_gain = jnp.sum(
        (mix_index[:, :, None] == table_index).astype(jnp.float32) * weight_table, axis=2
    )
    grown = []
    for channel in range(bond_local):
        mixed = (
            mix_gain[channel, 0] * rims[channel, 0].astype(jnp.float32)
            + mix_gain[channel, 1] * rims[channel + 1, 0].astype(jnp.float32)
            + mix_gain[channel, 2] * rims[channel + 2, 0].astype(jnp.float32)
        ).astype(jnp.bfloat16)
        half = jnp.dot(mixed, unit, preferred_element_type=jnp.float32).astype(jnp.bfloat16)
        outer = lax.dot_general(
            unit, half, (((0,), (0,)), ((), ())), preferred_element_type=jnp.float32
        )
        grown.append((outer / math.sqrt(states)).astype(jnp.bfloat16))
    env_next = jnp.stack(grown)[:, None]
    return (matvec, env_next)


def solution(mesh):
    split = Mesh(mesh.devices.reshape(4, 4, 4, 2), ("bond_0", "bond_1", "sector_0", "sector_1"))
    in_specs = (
        P(SECTOR, None, None),
        P(SECTOR),
        P(SECTOR),
        P(BOND, SECTOR, None, None),
        P(BOND, SECTOR, None, None),
        P(BOND),
        P(BOND),
        P(BOND, None),
        P(),
    )
    out_specs = (P(SECTOR, BOND, None), P(BOND, SECTOR, None, None))
    return jax.shard_map(
        on_device, mesh=split, in_specs=in_specs, out_specs=out_specs, check_vma=False
    )
```

profile of v0, /device:TPU:4, one launch (start us, length us, event | category | flops | bytes accessed | tf_op | source)
XLA Modules:
  0.0 157.8 jit_solution(4985551446748919577)
XLA Ops:
  1.9 0.7 convert_multiply_fusion.4
  2.6 0.6 fusion.61
  3.2 6.2 %fusion.15 = f32[768,768]{1,0:T(8,128)} fusion(bf16[2,1,768,768]{3,2,1,0:T(8,128)(2,1)} %param.13, bf16[1,768,768]{2,1,0:T(8,128)(2,1)} %param.9, pred[768]{0:T(1024)(128)(4,1)S(1)} %get-tuple-element.16, pred[768]{0:T(1024)(128)(4,1)S(1)} %get-tuple-element.17, bf16[2,1,768,768]{3,2,1,0:T(8,128)(2,1)} %param.12), kind=kOutput, calls=%fused_computation.26 | convolution fusion | flops 1813708800 | bytes 5899776 | tf_op jit(solution)/shard_map/dot_general | solution.py:80
  9.5 0.0 copy-done
  9.5 0.0 copy-done.4
  9.5 7.4 %multiply_add_fusion = f32[768,768]{1,0:T(8,128)} fusion(f32[768,768]{1,0:T(8,128)} %fusion.15, bf16[2,1,768,768]{3,2,1,0:T(8,128)(2,1)} %param.13, f32[]{:T(128)} %bitcast.6, f32[]{:T(128)} %bitcast, bf16[1,768,768]{2,1,0:T(8,128)(2,1)S(1)} %copy-done.4, pred[768]{0:T(1024)(128)(4,1)S(1)} %get-tuple-element.16, pred[768]{0:T(1024)(128)(4,1)S(1)} %get-tuple-element.17, ...), kind=kOutput, calls=%fused_computation.13 | convolution fusion | flops 1815478272 | bytes 8260608 | tf_op jit(solution)/shard_map/dot_general | solution.py:80
  16.8 8.3 %all-to-all-start = ((f32[16,48,768]{2,1,0:T(8,128)}), f32[16,48,768]{2,1,0:T(8,128)S(1)}, u32[]{:S(2)}, u32[]{:S(2)}) async-start(f32[16,48,768]{2,1,0:T(8,128)} %bitcast.66), calls=%async_computation | async-start | bytes 4718592 | tf_op jit(solution)/shard_map/all_to_all | solution.py:35
  25.2 0.1 dynamic_slice.3
  25.2 31.2 %all-to-all-done = f32[16,48,768]{2,1,0:T(8,128)S(1)} async-done(((f32[16,48,768]{2,1,0:T(8,128)}), f32[16,48,768]{2,1,0:T(8,128)S(1)}, u32[]{:S(2)}, u32[]{:S(2)}) %all-to-all-start) | async-done | bytes 2359328 | tf_op jit(solution)/shard_map/all_to_all | solution.py:35
  56.4 0.1 reduce_sum.29
  56.5 0.7 multiply_reduce_fusion
  57.2 8.5 %psum.28 = f32[]{:T(128)} all-reduce(f32[]{:T(128)} %multiply_reduce_fusion), channel_id=1, replica_groups=mesh['bond_0'=4,'bond_1'=4,'sector_0'=4,'sector_1'=2] {'bond_0'}, use_global_device_ids=true, to_apply=%region_2.3 | all-reduce | flops 1 | bytes 8 | tf_op jit(solution)/shard_map/psum | solution.py:41
  65.7 8.9 %psum.29 = f32[]{:T(128)} all-reduce(f32[]{:T(128)} %psum.28), channel_id=1, replica_groups=mesh['bond_0'=4,'bond_1'=4,'sector_0'=4,'sector_1'=2] {'bond_1'}, use_global_device_ids=true, to_apply=%region_3.4 | all-reduce | flops 1 | bytes 8 | tf_op jit(solution)/shard_map/psum | solution.py:41
  74.6 3.2 %fusion.59 = (bf16[1,1,768,768]{3,2,1,0:T(8,128)(2,1)}, bf16[1,1,768,768]{3,2,1,0:T(8,128)(2,1)}) fusion(bf16[2,1,768,768]{3,2,1,0:T(8,128)(2,1)} %param.12), kind=kLoop, calls=%fused_computation.58 | loop fusion | bytes 4718592 | tf_op jit(solution)/shard_map/slice | solution.py:78
  77.8 11.4 %psum.30 = f32[]{:T(128)} all-reduce(f32[]{:T(128)} %psum.29), channel_id=1, replica_groups=mesh['bond_0'=4,'bond_1'=4,'sector_0'=4,'sector_1'=2] {'sector_0'}, use_global_device_ids=true, to_apply=%region_4.5 | all-reduce | flops 1 | bytes 8 | tf_op jit(solution)/shard_map/psum | solution.py:41
  89.2 5.7 %collective-permute-start.1 = (bf16[1,1,768,768]{3,2,1,0:T(8,128)(2,1)}, bf16[1,1,768,768]{3,2,1,0:T(8,128)(2,1)}, u32[]{:S(2)}, u32[]{:S(2)}) collective-permute-start(bf16[1,1,768,768]{3,2,1,0:T(8,128)(2,1)} %get-tuple-element.7), channel_id=1, source_target_pairs={{8,0},{16,8},{24,16},{32,24},{40,32},{48,40},{56,48},{64,56},{72,6... | collective-permute-start | bytes 3538952 | tf_op jit(solution)/shard_map/ppermute | solution.py:22
  94.9 3.1 %psum.31 = f32[]{:T(128)} all-reduce(f32[]{:T(128)} %psum.30), channel_id=1, replica_groups=mesh['bond_0'=4,'bond_1'=4,'sector_0'=4,'sector_1'=2] {'sector_1'}, use_global_device_ids=true, to_apply=%region_5.6 | all-reduce | flops 1 | bytes 8 | tf_op jit(solution)/shard_map/psum | solution.py:41
  98.7 0.1 multiply_convert_fusion.2
  98.8 1.1 broadcast_in_dim.7
  99.9 5.0 %all-to-all-start.1 = ((bf16[16,48,768]{2,1,0:T(8,128)(2,1)}), bf16[16,48,768]{2,1,0:T(8,128)(2,1)}, u32[]{:S(2)}, u32[]{:S(2)}) async-start(bf16[16,48,768]{2,1,0:T(8,128)(2,1)} %broadcast_in_dim.7), calls=%async_computation.1 | async-start | bytes 2359296 | tf_op jit(solution)/shard_map/all_to_all | solution.py:53
  104.8 3.5 %collective-permute-start = (bf16[1,1,768,768]{3,2,1,0:T(8,128)(2,1)}, bf16[1,1,768,768]{3,2,1,0:T(8,128)(2,1)}, u32[]{:S(2)}, u32[]{:S(2)}) collective-permute-start(bf16[1,1,768,768]{3,2,1,0:T(8,128)(2,1)} %get-tuple-element.6), channel_id=1, source_target_pairs={{0,8},{8,16},{16,24},{24,32},{32,40},{40,48},{48,56},{56,64},{64,7... | collective-permute-start | bytes 3538952 | tf_op jit(solution)/shard_map/ppermute | solution.py:21
  108.4 0.0 copy-done.2
  108.4 0.1 copy.12
  108.5 0.2 fusion.40
  108.6 0.7 fusion.60
  109.3 0.7 fusion.39
  110.0 14.2 %collective-permute-done.1 = bf16[1,1,768,768]{3,2,1,0:T(8,128)(2,1)} collective-permute-done((bf16[1,1,768,768]{3,2,1,0:T(8,128)(2,1)}, bf16[1,1,768,768]{3,2,1,0:T(8,128)(2,1)}, u32[]{:S(2)}, u32[]{:S(2)}) %collective-permute-start.1) | collective-permute-done | bytes 1179680 | tf_op jit(solution)/shard_map/ppermute | solution.py:22
  124.2 2.4 %all-to-all-done.1 = bf16[16,48,768]{2,1,0:T(8,128)(2,1)} async-done(((bf16[16,48,768]{2,1,0:T(8,128)(2,1)}), bf16[16,48,768]{2,1,0:T(8,128)(2,1)}, u32[]{:S(2)}, u32[]{:S(2)}) %all-to-all-start.1) | async-done | bytes 1179680 | tf_op jit(solution)/shard_map/all_to_all | solution.py:53
  126.6 7.3 %fusion.7 = bf16[1,768,768]{2,1,0:T(8,128)(2,1)S(1)} fusion(bf16[768,768]{1,0:T(8,128)(2,1)} %bitcast.11, bf16[1,1,768,768]{3,2,1,0:T(8,128)(2,1)} %collective-permute-done.1, f32[]{:T(128)} %bitcast.19, f32[]{:T(128)} %bitcast.18, f32[]{:T(128)} %bitcast.17, bf16[2,1,768,768]{3,2,1,0:T(8,128)(2,1)S(1)} %copy-done.1), kind=kOutput, calls=%fused_computation.20 | convolution fusion | flops 1819017216 | bytes 7079424 | tf_op jit(solution)/shard_map/dot_general | solution.py:106
  133.9 12.7 %collective-permute-done = bf16[1,1,768,768]{3,2,1,0:T(8,128)(2,1)} collective-permute-done((bf16[1,1,768,768]{3,2,1,0:T(8,128)(2,1)}, bf16[1,1,768,768]{3,2,1,0:T(8,128)(2,1)}, u32[]{:S(2)}, u32[]{:S(2)}) %collective-permute-start) | collective-permute-done | bytes 1179680 | tf_op jit(solution)/shard_map/ppermute | solution.py:21
  146.6 8.3 %fusion.6 = bf16[1,768,768]{2,1,0:T(8,128)(2,1)} fusion(bf16[768,768]{1,0:T(8,128)(2,1)} %bitcast.11, bf16[1,1,768,768]{3,2,1,0:T(8,128)(2,1)} %collective-permute-done, f32[]{:T(128)} %bitcast.14, f32[]{:T(128)} %bitcast.13, f32[]{:T(128)} %bitcast.12, bf16[2,1,768,768]{3,2,1,0:T(8,128)(2,1)S(1)} %copy-done.1), kind=kOutput, calls=%fused_computation.19 | convolution fusion | flops 1819017216 | bytes 7079424 | tf_op jit(solution)/shard_map/dot_general | solution.py:106
  154.9 2.9 %maximum_bitcast_fusion = bf16[2,1,768,768]{3,2,1,0:T(8,128)(2,1)} fusion(bf16[1,768,768]{2,1,0:T(8,128)(2,1)S(1)} %fusion.7, bf16[1,768,768]{2,1,0:T(8,128)(2,1)} %fusion.6), kind=kLoop, calls=%fused_computation.10 | loop fusion | flops 1179648 | bytes 4718592
  (10 shorter events, 0.0 us)
Async XLA Ops:
  3.2 6.3 %copy-start = (bf16[2,1,768,768]{3,2,1,0:T(8,128)(2,1)S(1)}, bf16[2,1,768,768]{3,2,1,0:T(8,128)(2,1)}, u32[]{:S(2)}) copy-start(bf16[2,1,768,768]{3,2,1,0:T(8,128)(2,1)} %param.12) | copy-start | bytes 7077892
  3.2 6.3 %copy-start.4 = (bf16[1,768,768]{2,1,0:T(8,128)(2,1)S(1)}, bf16[1,768,768]{2,1,0:T(8,128)(2,1)}, u32[]{:S(2)}) copy-start(bf16[1,768,768]{2,1,0:T(8,128)(2,1)} %param.9) | copy-start | bytes 3538948
  16.8 39.6 %all-to-all-start = ((f32[16,48,768]{2,1,0:T(8,128)}), f32[16,48,768]{2,1,0:T(8,128)S(1)}, u32[]{:S(2)}, u32[]{:S(2)}) async-start(f32[16,48,768]{2,1,0:T(8,128)} %bitcast.66), calls=%async_computation | async-start | bytes 4718592 | tf_op jit(solution)/shard_map/all_to_all | solution.py:35
  89.2 35.1 %collective-permute-start.1 = (bf16[1,1,768,768]{3,2,1,0:T(8,128)(2,1)}, bf16[1,1,768,768]{3,2,1,0:T(8,128)(2,1)}, u32[]{:S(2)}, u32[]{:S(2)}) collective-permute-start(bf16[1,1,768,768]{3,2,1,0:T(8,128)(2,1)} %get-tuple-element.7), channel_id=1, source_target_pairs={{8,0},{16,8},{24,16},{32,24},{40,32},{48,40},{56,48},{64,56},{72,6... | collective-permute-start | bytes 3538952 | tf_op jit(solution)/shard_map/ppermute | solution.py:22
  99.8 8.5 %copy-start.2 = (s32[2,3]{1,0:T(2,128)S(1)}, s32[2,3]{1,0:T(2,128)}, u32[]{:S(2)}) copy-start(s32[2,3]{1,0:T(2,128)} %param.16) | copy-start | bytes 76
  99.8 8.6 %copy-start.3 = (f32[8]{0:T(128)S(1)}, f32[8]{0:T(128)}, u32[]{:S(2)}) copy-start(f32[8]{0:T(128)} %param.17) | copy-start | bytes 100
  99.9 26.8 %copy-start.1 = (bf16[2,1,768,768]{3,2,1,0:T(8,128)(2,1)S(1)}, bf16[2,1,768,768]{3,2,1,0:T(8,128)(2,1)}, u32[]{:S(2)}) copy-start(bf16[2,1,768,768]{3,2,1,0:T(8,128)(2,1)} %param.12) | copy-start | bytes 7077892
  99.9 26.8 %all-to-all-start.1 = ((bf16[16,48,768]{2,1,0:T(8,128)(2,1)}), bf16[16,48,768]{2,1,0:T(8,128)(2,1)}, u32[]{:S(2)}, u32[]{:S(2)}) async-start(bf16[16,48,768]{2,1,0:T(8,128)(2,1)} %broadcast_in_dim.7), calls=%async_computation.1 | async-start | bytes 2359296 | tf_op jit(solution)/shard_map/all_to_all | solution.py:53
  104.8 41.8 %collective-permute-start = (bf16[1,1,768,768]{3,2,1,0:T(8,128)(2,1)}, bf16[1,1,768,768]{3,2,1,0:T(8,128)(2,1)}, u32[]{:S(2)}, u32[]{:S(2)}) collective-permute-start(bf16[1,1,768,768]{3,2,1,0:T(8,128)(2,1)} %get-tuple-element.6), channel_id=1, source_target_pairs={{0,8},{8,16},{16,24},{24,32},{32,40},{40,48},{48,56},{56,64},{64,7... | collective-permute-start | bytes 3538952 | tf_op jit(solution)/shard_map/ppermute | solution.py:21
where the time goes:
time: 158 us
  waiting for transfers between devices  60.4 us (38%)
  blocking collectives  31.9 us (20%)
  matrix products  29.2 us (18%)
  starting transfers between devices  22.5 us (14%)
  local copies, waits for them, and re-layouts  5.75 us (4%)
  other arithmetic  5.37 us (3%)
  between operations  2.67 us (2%)
    psum x4, blocking collectives, one_axis_at_a_time(): shard = lax.psum(shard, axis)  31.9 us
    all_to_all x1, waiting for transfers between devices, sum_at_owner(): lax.all_to_all(parts, axis, split_axis=0, concat_axis=0, tiled=True)  31.2 us
    dot_general x2, matrix products, on_device(): lax.dot_general(unit, half, (((0,), (0,)), ((), ())), preferred_element_t...  15.6 us
    ppermute x1, waiting for transfers between devices, padded(): after = lax.ppermute(first, axis, down)  14.2 us
    dot_general x2, matrix products, on_device(): lax.dot_general(applied, env_right[term_channel, 0], (((1,), (1,)), ((),...  13.6 us
    ppermute x1, waiting for transfers between devices, padded(): before = lax.ppermute(last, axis, up)  12.7 us
    all_to_all x1, starting transfers between devices, sum_at_owner(): lax.all_to_all(parts, axis, split_axis=0, concat_axis=0, tiled=True)  8.3 us
    ppermute x1, starting transfers between devices, padded(): after = lax.ppermute(first, axis, down)  5.67 us
  transfers between devices with their start and end apart: 4, of which 4 were waited for; matrix products, arithmetic and copies ran while one was open for 6% of the time, Pallas kernels for 0%

commit v1 on v0

v1 whole, which is shorter than its diff:
```python
import math

import jax
import jax.numpy as jnp
from jax import lax
from jax.experimental import pallas as pl
from jax.experimental.pallas import tpu as pltpu
from jax.sharding import Mesh
from jax.sharding import PartitionSpec as P

AXES = ("bond_0", "bond_1", "sector_0", "sector_1")
BOND = ("bond_0", "bond_1")
SECTOR = ("sector_0", "sector_1")
MESH = pl.DeviceIdType.MESH
F32 = jnp.float32
BF16 = jnp.bfloat16

N = 768
BLK = 48
PIECES = 6
EARLY = 4
PIECE = N // PIECES
TILE = 256

RELAY_UP, RELAY_DOWN, UP_B, DOWN_A, UP_A, DOWN_B = range(6)
RS_Z = 6
AG_Z = 9
AG_UP = 12
AG_DOWN = 16
FWD = 20
SUM_CORE = 24
SUM_Y = 25
SUM_X = 28
SUM_Z = 31
HALO_UP = 34
HALO_DOWN = HALO_UP + PIECES
COPIES = HALO_DOWN + PIECES


def body(
    theta_h, left_h, right_h, rows_s, cols_s, on_s, coef_s, index_s, table_s,
    matvec_o, env_o,
    live, left, right, low, high, acc, relay_out, relay_in, side_out, from_left, from_right,
    z_out, z_in, unit, part, part_in, mixed, half, grown,
    load_sem, send_sem, recv_sem, store_sem,
):
    x = lax.axis_index("bond_0")
    z = lax.axis_index("bond_1")
    y = lax.axis_index("sector_0")
    c = lax.axis_index("sector_1")

    def at_x(d):
        return {"bond_0": lax.rem(x + d, 4)}

    def at_z(d):
        return {"bond_1": lax.rem(z + d, 4)}

    def at_y(d):
        return {"sector_0": lax.rem(y + d, 4)}

    other = {"sector_1": 1 - c}
    bond = x * 4 + z
    above = lax.rem(bond + 1, 16)
    below = lax.rem(bond + 15, 16)
    up = {"bond_0": above // 4, "bond_1": lax.rem(above, 4)}
    down = {"bond_0": below // 4, "bond_1": lax.rem(below, 4)}
    peers = [at_x(1), at_x(2), at_x(3), at_z(1), at_z(2), at_z(3), at_y(1), at_y(2), at_y(3), other, up, down]

    def remote(i, src, dst, device):
        return pltpu.make_async_remote_copy(
            src_ref=src, dst_ref=dst, send_sem=send_sem.at[i], recv_sem=recv_sem.at[i],
            device_id=device, device_id_type=MESH,
        )

    loads = [
        pltpu.make_async_copy(theta_h.at[0], live, load_sem.at[0]),
        pltpu.make_async_copy(left_h.at[0, 0], left.at[0], load_sem.at[1]),
        pltpu.make_async_copy(left_h.at[1, 0], left.at[1], load_sem.at[2]),
        pltpu.make_async_copy(right_h.at[0, 0], right.at[0], load_sem.at[3]),
        pltpu.make_async_copy(right_h.at[1, 0], right.at[1], load_sem.at[4]),
    ]
    barrier = pltpu.get_barrier_semaphore()
    for peer in peers:
        pl.semaphore_signal(barrier, inc=1, device_id=peer, device_id_type=MESH)
    for load in loads:
        load.start()
    pl.semaphore_wait(barrier, len(peers))

    def halo_up(p):
        rows = pl.ds(p * PIECE, PIECE)
        return remote(HALO_UP + p, left_h.at[1, 0, rows], low.at[rows], up)

    def halo_down(p):
        rows = pl.ds(p * PIECE, PIECE)
        return remote(HALO_DOWN + p, left_h.at[0, 0, rows], high.at[rows], down)

    for p in range(EARLY):
        halo_up(p).start()
        halo_down(p).start()

    row_dim = rows_s[0]
    col_dim = cols_s[0]
    loads[0].wait()

    @pl.loop(0, N // 128)
    def _(i):
        rows = pl.ds(pl.multiple_of(i * 128, 128), 128)
        row_id = lax.broadcasted_iota(jnp.int32, (128, N), 0) + i * 128
        col_id = lax.broadcasted_iota(jnp.int32, (128, N), 1)
        keep = (row_id < row_dim) & (col_id < col_dim)
        live[rows] = jnp.where(keep, live[rows].astype(F32), 0.0).astype(BF16)

    for load in loads[1:]:
        load.wait()

    gains = [coef_s[w] * on_s[w].astype(F32) for w in range(2)]

    relay_up = remote(RELAY_UP, relay_out.at[0], relay_in.at[0], at_x(1))
    relay_down = remote(RELAY_DOWN, relay_out.at[1], relay_in.at[1], at_x(3))
    up_b = remote(UP_B, side_out.at[0, pl.ds(2, 2)], from_left.at[pl.ds(2, 2)], at_x(1))
    up_a = remote(UP_A, side_out.at[0, pl.ds(0, 2)], from_left.at[pl.ds(0, 2)], at_x(1))
    down_a = remote(DOWN_A, side_out.at[1, pl.ds(0, 2)], from_right.at[pl.ds(0, 2)], at_x(3))
    down_b = remote(DOWN_B, side_out.at[1, pl.ds(2, 2)], from_right.at[pl.ds(2, 2)], at_x(3))

    @pl.loop(0, 4)
    def _(i):
        owner = lax.rem(x + 2 + i, 4)
        rows = pl.ds(pl.multiple_of(owner * 192, 64), 192)
        total = None
        for w in range(2):
            applied = jnp.dot(left[w, rows, :], live[...], preferred_element_type=F32).astype(BF16)
            term = gains[w] * lax.dot_general(
                applied, right[w], (((1,), (1,)), ((), ())), preferred_element_type=F32
            )
            total = term if total is None else total + term
        acc[i] = total.reshape(4, BLK, N)

        @pl.when(i == 0)
        def _():
            relay_out[0] = acc[0, 0:2].astype(BF16)
            relay_up.start()
            relay_out[1] = acc[0, 2:4].astype(BF16)
            relay_down.start()

        @pl.when(i == 1)
        def _():
            side_out[1, 0:2] = acc[1, 0:2].astype(BF16)
            down_a.start()

        @pl.when(i == 3)
        def _():
            side_out[0, 2:4] = acc[3, 2:4].astype(BF16)
            up_b.start()

    relay_up.wait_recv()
    side_out[0, 0:2] = (acc[3, 0:2] + relay_in[0].astype(F32)).astype(BF16)
    up_a.start()
    relay_down.wait_recv()
    side_out[1, 2:4] = (acc[1, 2:4] + relay_in[1].astype(F32)).astype(BF16)
    down_b.start()

    up_b.wait_recv()
    down_a.wait_recv()
    up_a.wait_recv()
    down_b.wait_recv()

    def row_sum(j):
        return acc[2, j] + from_left[j].astype(F32) + from_right[j].astype(F32)

    rs_z = {d: remote(RS_Z + d - 1, z_out.at[d - 1], z_in.at[d - 1], at_z(d)) for d in (1, 2, 3)}
    for d in (2, 1, 3):
        z_out[d - 1] = row_sum(lax.rem(z + d, 4)).astype(BF16)
        rs_z[d].start()
    mine = row_sum(z)
    for d in (1, 3, 2):
        rs_z[d].wait_recv()
        mine = mine + z_in[d - 1].astype(F32)
    row_id = lax.broadcasted_iota(jnp.int32, (BLK, N), 0) + bond * BLK
    col_id = lax.broadcasted_iota(jnp.int32, (BLK, N), 1)
    mine = jnp.where((row_id < row_dim) & (col_id < col_dim), mine, 0.0)
    rounded = mine.astype(BF16)
    unit[bond] = rounded

    def block(cx, r):
        return unit.at[lax.rem(x + cx, 4) * 4 + lax.rem(z + 4 - r, 4)]

    ag_z = {d: remote(AG_Z + d - 1, unit.at[bond], unit.at[bond], at_z(d)) for d in (1, 2, 3)}
    for d in (2, 1, 3):
        ag_z[d].start()
    ag_up = [remote(AG_UP + r, block(0, r), block(0, r), at_x(1)) for r in range(4)]
    ag_down = [remote(AG_DOWN + r, block(0, r), block(0, r), at_x(3)) for r in range(4)]
    ag_up[0].start()
    ag_down[0].start()

    matvec_o[...] = rounded
    square = mine * mine
    tile = jnp.zeros((8, 128), F32)
    for a in range(BLK // 8):
        for b in range(N // 128):
            tile = tile + square[a * 8 : a * 8 + 8, b * 128 : b * 128 + 128]
    part[0] = tile

    def spread(i, slot, devices):
        return [
            remote(i + n, part.at[slot], part_in.at[i - SUM_CORE + n], device) for n, device in enumerate(devices)
        ]

    sums = [
        spread(SUM_CORE, 0, [other]),
        spread(SUM_Y, 1, [at_y(1), at_y(2), at_y(3)]),
        spread(SUM_X, 2, [at_x(1), at_x(2), at_x(3)]),
        spread(SUM_Z, 3, [at_z(1), at_z(2), at_z(3)]),
    ]
    firsts = [0, 1, 4, 7]

    def sum_start(stage):
        for copy in sums[stage]:
            copy.start()

    def sum_finish(stage):
        total = part[stage]
        for n, copy in enumerate(sums[stage]):
            copy.wait_recv()
            total = total + part_in[firsts[stage] + n]
        part[stage + 1] = total

    sum_start(0)
    for d in (1, 3, 2):
        remote(AG_Z + d - 1, block(0, d), block(0, d), at_z(d)).wait_recv()
        ag_up[d].start()
        ag_down[d].start()
    for p in range(EARLY, PIECES):
        halo_up(p).start()
        halo_down(p).start()
    sum_finish(0)
    sum_start(1)

    w_gain = [[table_s[index_s[w, k]] for k in range(3)] for w in range(2)]
    low_gain = jnp.where(bond > 0, w_gain[0][0], 0.0)
    high_gain = jnp.where(bond < 15, w_gain[1][2], 0.0)

    def mix(p):
        rows = pl.ds(p * PIECE, PIECE)
        halo_up(p).wait_recv()
        halo_down(p).wait_recv()
        here = left[0, rows].astype(F32)
        there = left[1, rows].astype(F32)
        mixed[0, rows] = (low_gain * low[rows].astype(F32) + w_gain[0][1] * here + w_gain[0][2] * there).astype(BF16)
        mixed[1, rows] = (w_gain[1][0] * here + w_gain[1][1] * there + high_gain * high[rows].astype(F32)).astype(BF16)

    def arrive(i, cx, r):
        remote(i + r, block(cx, r), block(cx, r), at_x(1)).wait_recv()

    fwd = {
        0: remote(FWD, block(3, 0), block(3, 0), at_x(1)),
        3: remote(FWD + 3, block(3, 3), block(3, 3), at_x(1)),
        1: remote(FWD + 1, block(1, 1), block(1, 1), at_x(3)),
        2: remote(FWD + 2, block(1, 2), block(1, 2), at_x(3)),
    }
    arrive(AG_UP, 3, 0)
    fwd[0].start()
    arrive(AG_DOWN, 1, 0)
    arrive(AG_DOWN, 1, 1)
    fwd[1].start()
    arrive(AG_UP, 3, 1)
    sum_finish(1)
    sum_start(2)
    arrive(AG_UP, 3, 3)
    fwd[3].start()
    arrive(AG_DOWN, 1, 3)
    arrive(AG_DOWN, 1, 2)
    fwd[2].start()
    arrive(AG_UP, 3, 2)
    sum_finish(2)
    sum_start(3)
    for p in range(EARLY):
        mix(p)
    sum_finish(3)
    square_total = jnp.sum(part[4])
    scale = lax.rsqrt(jnp.full((1, N), square_total * (1.0 / (8 * N * N)) + 1e-06, F32))
    for p in range(EARLY, PIECES):
        mix(p)
    for r in range(4):
        remote(FWD + r, block(2, r), block(2, r), at_x(1)).wait_recv()

    @pl.loop(0, 2)
    def _(w):
        for k in range(N // TILE):
            rows = pl.ds(k * TILE, TILE)
            product = jnp.dot(mixed[w, rows, :], unit[...].reshape(N, N), preferred_element_type=F32)
            half[rows] = (product * scale).astype(BF16)
        for k in range(N // TILE):
            rows = pl.ds(k * TILE, TILE)
            side = unit[:, :, k * TILE : (k + 1) * TILE].reshape(N, TILE)
            product = lax.dot_general(side, half[...], (((0,), (0,)), ((), ())), preferred_element_type=F32)
            grown[w, rows] = (product * (scale * (1.0 / math.sqrt(N)))).astype(BF16)
        pltpu.make_async_copy(grown.at[w], env_o.at[w, 0], store_sem.at[w]).start()

    for copy in (relay_up, relay_down, up_a, up_b, down_a, down_b):
        copy.wait_send()
    for d in (1, 2, 3):
        rs_z[d].wait_send()
        ag_z[d].wait_send()
    for r in range(4):
        ag_up[r].wait_send()
        ag_down[r].wait_send()
        fwd[r].wait_send()
    for stage in sums:
        for copy in stage:
            copy.wait_send()
    for p in range(PIECES):
        halo_up(p).wait_send()
        halo_down(p).wait_send()
    for w in range(2):
        pltpu.make_async_copy(grown.at[w], env_o.at[w, 0], store_sem.at[w]).wait()


def on_device(
    theta, sector_dims, right_dims, env_left, env_right, mpo_on, mpo_coef, mix_index, weight_table
):
    hbm = pl.BlockSpec(memory_space=pl.ANY)
    smem = pl.BlockSpec(memory_space=pltpu.SMEM)
    matvec, env_next = pl.pallas_call(
        body,
        out_shape=(
            jax.ShapeDtypeStruct((BLK, N), BF16),
            jax.ShapeDtypeStruct(env_left.shape, BF16),
        ),
        in_specs=[hbm, hbm, hbm, smem, smem, smem, smem, smem, smem],
        out_specs=(pl.BlockSpec(memory_space=pltpu.VMEM), hbm),
        scratch_shapes=[
            pltpu.VMEM((N, N), BF16),
            pltpu.VMEM((2, N, N), BF16),
            pltpu.VMEM((2, N, N), BF16),
            pltpu.VMEM((N, N), BF16),
            pltpu.VMEM((N, N), BF16),
            pltpu.VMEM((4, 4, BLK, N), F32),
            pltpu.VMEM((2, 2, BLK, N), BF16),
            pltpu.VMEM((2, 2, BLK, N), BF16),
            pltpu.VMEM((2, 4, BLK, N), BF16),
            pltpu.VMEM((4, BLK, N), BF16),
            pltpu.VMEM((4, BLK, N), BF16),
            pltpu.VMEM((3, BLK, N), BF16),
            pltpu.VMEM((3, BLK, N), BF16),
            pltpu.VMEM((16, BLK, N), BF16),
            pltpu.VMEM((5, 8, 128), F32),
            pltpu.VMEM((10, 8, 128), F32),
            pltpu.VMEM((2, N, N), BF16),
            pltpu.VMEM((N, N), BF16),
            pltpu.VMEM((2, N, N), BF16),
            pltpu.SemaphoreType.DMA((5,)),
            pltpu.SemaphoreType.DMA((COPIES,)),
            pltpu.SemaphoreType.DMA((COPIES,)),
            pltpu.SemaphoreType.DMA((2,)),
        ],
        compiler_params=pltpu.CompilerParams(
            collective_id=0, has_side_effects=True, vmem_limit_bytes=56 * 1024 * 1024
        ),
        name="sweep",
    )(theta, env_left, env_right, sector_dims, right_dims, mpo_on, mpo_coef, mix_index, weight_table)
    return (matvec[None], env_next)


def solution(mesh):
    split = Mesh(mesh.devices.reshape(4, 4, 4, 2), AXES)
    in_specs = (
        P(SECTOR, None, None),
        P(SECTOR),
        P(SECTOR),
        P(BOND, SECTOR, None, None),
        P(BOND, SECTOR, None, None),
        P(BOND),
        P(BOND),
        P(BOND, None),
        P(),
    )
    out_specs = (P(SECTOR, BOND, None), P(BOND, SECTOR, None, None))
    return jax.shard_map(on_device, mesh=split, in_specs=in_specs, out_specs=out_specs, check_vma=False)
```

time: 158 us -> 77.3 us (0.49)
  the two profiles are of different devices: /device:TPU:4 before, /device:TPU:0 now
where the time goes in v1:
time: 77.3 us; the launch traced here: 76.6 us
  Pallas kernels  69.9 us (90%)
  local copies, waits for them, and re-layouts  4.74 us (6%)
  between operations  1.93 us (2%)
    pallas_call x1, Pallas kernels, on_device(): pl.pallas_call(body, out_shape=(jax.ShapeDtypeStruct((BLK, N), BF16), jax...  69.9 us
    unnamed x2, local copies, waits for them, and re-layouts  4.74 us

profile of v1, /device:TPU:0, one launch (start us, length us, event | category | flops | bytes accessed | tf_op | source)
XLA Modules:
  0.0 76.6 jit_solution(14079467950234937840)
XLA Ops:
  1.9 69.9 %sweep.1 = (bf16[48,768]{1,0:T(8,128)(2,1)}, bf16[2,1,768,768]{3,2,1,0:T(8,128)(2,1)}) custom-call(bf16[1,768,768]{2,1,0:T(8,128)(2,1)} %theta_h.1, bf16[2,1,768,768]{3,2,1,0:T(8,128)(2,1)} %left_h.1, bf16[2,1,768,768]{3,2,1,0:T(8,128)(2,1)} %right_h.1, s32[1]{0:T(128)S(6)} %copy.13.rows_s, s32[1]{0:T(128)S(6)} %copy.14.cols_s, s32[2]{0:T(128)} %on_s.1, ...), custom_call_target="tpu_custom_call" | custom-call | tf_op jit(solution)/shard_map/sweep/pallas_call | solution.py:323
  71.8 1.5 %copy.15 = bf16[1,48,768]{2,1,0:T(8,128)(2,1)} copy(bf16[1,48,768]{2,1,0:T(8,128)(2,1)} %bitcast.1) | data formatting | bytes 147456
  73.4 3.2 %copy.16 = bf16[2,1,768,768]{3,2,1,0:T(8,128)(2,1)} copy(bf16[2,1,768,768]{3,2,1,0:T(8,128)(2,1)} %get-tuple-element.9) | data formatting | bytes 4718592

commit v2 on v1

--- a/solution.py
+++ b/solution.py
@@ -19,6 +19,8 @@
 BLK = 48
 PIECES = 6
 EARLY = 4
+HOPS = 3
+ORDER = (3, 0, 1, 4, 5, 2)
 PIECE = N // PIECES
 TILE = 256
 
@@ -34,15 +36,18 @@
 SUM_Z = 31
 HALO_UP = 34
 HALO_DOWN = HALO_UP + PIECES
-COPIES = HALO_DOWN + PIECES
+HOP_UP = HALO_DOWN + PIECES
+HOP_DOWN = HOP_UP + HOPS
+COPIES = HOP_DOWN + HOPS
 
 
 def body(
-    theta_h, left_h, right_h, rows_s, cols_s, on_s, coef_s, index_s, table_s,
-    matvec_o, env_o,
-    live, left, right, low, high, acc, relay_out, relay_in, side_out, from_left, from_right,
-    z_out, z_in, unit, part, part_in, mixed, half, grown,
-    load_sem, send_sem, recv_sem, store_sem,
+    theta_h, left_h, right_h, rows_h, cols_h, on_h, coef_h, index_h, table_h,
+    matvec_o, half_o, unit_o, square_o,
+    rows_s, cols_s, on_s, coef_s, index_s, table_s,
+    live, left, right, low, high, via_up, via_down, acc, relay_out, relay_in, side_out, from_left, from_right,
+    z_out, z_in, unit, part, part_in, mixed, half,
+    small_sem, load_sem, send_sem, recv_sem, store_sem,
 ):
     x = lax.axis_index("bond_0")
     z = lax.axis_index("bond_1")
@@ -79,25 +84,77 @@
         pltpu.make_async_copy(right_h.at[0, 0], right.at[0], load_sem.at[3]),
         pltpu.make_async_copy(right_h.at[1, 0], right.at[1], load_sem.at[4]),
     ]
+    smalls = [
+        pltpu.make_async_copy(source, target, small_sem.at[n])
+        for n, (source, target) in enumerate(
+            [(rows_h, rows_s), (cols_h, cols_s), (on_h, on_s), (coef_h, coef_s), (index_h, index_s), (table_h, table_s)]
+        )
+    ]
     barrier = pltpu.get_barrier_semaphore()
     for peer in peers:
         pl.semaphore_signal(barrier, inc=1, device_id=peer, device_id_type=MESH)
-    for load in loads:
+    for load in smalls + loads:
         load.start()
     pl.semaphore_wait(barrier, len(peers))
 
-    def halo_up(p):
-        rows = pl.ds(p * PIECE, PIECE)
-        return remote(HALO_UP + p, left_h.at[1, 0, rows], low.at[rows], up)
-
-    def halo_down(p):
-        rows = pl.ds(p * PIECE, PIECE)
-        return remote(HALO_DOWN + p, left_h.at[0, 0, rows], high.at[rows], down)
+    def rows_of(p):
+        return pl.ds(p * PIECE, PIECE)
+
+    def up_first(p, via):
+        target = via_up.at[p] if via else low.at[rows_of(p)]
+        return remote(HALO_UP + p, left_h.at[1, 0, rows_of(p)], target, at_z(1) if p < HOPS else up)
+
+    def down_first(p, via):
+        target = via_down.at[p] if via else high.at[rows_of(p)]
+        return remote(HALO_DOWN + p, left_h.at[0, 0, rows_of(p)], target, at_z(3) if p < HOPS else down)
+
+    def up_hop(p):
+        return remote(HOP_UP + p, via_up.at[p], low.at[rows_of(p)], at_x(1))
+
+    def down_hop(p):
+        return remote(HOP_DOWN + p, via_down.at[p], high.at[rows_of(p)], at_x(3))
+
+    def start_up(p):
+        if p < HOPS:
+            pl.when(z == 3)(lambda: up_first(p, True).start())
+            pl.when(z != 3)(lambda: up_first(p, False).start())
+        else:
+            up_first(p, False).start()
+
+    def start_down(p):
+        if p < HOPS:
+            pl.when(z == 0)(lambda: down_first(p, True).start())
+            pl.when(z != 0)(lambda: down_first(p, False).start())
+        else:
+            down_first(p, False).start()
+
+    def forward(p):
+        @pl.when(z == 0)
+        def _():
+            up_first(p, True).wait_recv()
+            up_hop(p).start()
+
+        @pl.when(z == 3)
+        def _():
+            down_first(p, True).wait_recv()
+            down_hop(p).start()
+
+    def halo_arrive(p):
+        if p < HOPS:
+            pl.when(z == 0)(lambda: up_hop(p).wait_recv())
+            pl.when(z != 0)(lambda: up_first(p, False).wait_recv())
+            pl.when(z == 3)(lambda: down_hop(p).wait_recv())
+            pl.when(z != 3)(lambda: down_first(p, False).wait_recv())
+        else:
+            up_first(p, False).wait_recv()
+            down_first(p, False).wait_recv()
 
     for p in range(EARLY):
-        halo_up(p).start()
-        halo_down(p).start()
-
+        start_up(p)
+        start_down(p)
+
+    for load in smalls:
+        load.wait()
     row_dim = rows_s[0]
     col_dim = cols_s[0]
     loads[0].wait()
@@ -163,6 +220,19 @@
     down_a.wait_recv()
     up_a.wait_recv()
     down_b.wait_recv()
+
+    @pl.when(z == 3)
+    def _():
+        for p in range(EARLY, PIECES):
+            start_up(p)
+
+    @pl.when(z == 0)
+    def _():
+        for p in range(EARLY, PIECES):
+            start_down(p)
+
+    forward(0)
+    forward(1)
 
     def row_sum(j):
         return acc[2, j] + from_left[j].astype(F32) + from_right[j].astype(F32)
@@ -229,9 +299,17 @@
         remote(AG_Z + d - 1, block(0, d), block(0, d), at_z(d)).wait_recv()
         ag_up[d].start()
         ag_down[d].start()
-    for p in range(EARLY, PIECES):
-        halo_up(p).start()
-        halo_down(p).start()
+
+    @pl.when(z != 3)
+    def _():
+        for p in range(EARLY, PIECES):
+            start_up(p)
+
+    @pl.when(z != 0)
+    def _():
+        for p in range(EARLY, PIECES):
+            start_down(p)
+
     sum_finish(0)
     sum_start(1)
 
@@ -240,9 +318,8 @@
     high_gain = jnp.where(bond < 15, w_gain[1][2], 0.0)
 
     def mix(p):
-        rows = pl.ds(p * PIECE, PIECE)
-        halo_up(p).wait_recv()
-        halo_down(p).wait_recv()
+        rows = rows_of(p)
+        halo_arrive(p)
         here = left[0, rows].astype(F32)
         there = left[1, rows].astype(F32)
         mixed[0, rows] = (low_gain * low[rows].astype(F32) + w_gain[0][1] * here + w_gain[0][2] * there).astype(BF16)
@@ -273,28 +350,29 @@
     arrive(AG_UP, 3, 2)
     sum_finish(2)
     sum_start(3)
-    for p in range(EARLY):
+    forward(2)
+    for p in ORDER[:4]:
         mix(p)
     sum_finish(3)
+    square_o[...] = part[4]
     square_total = jnp.sum(part[4])
     scale = lax.rsqrt(jnp.full((1, N), square_total * (1.0 / (8 * N * N)) + 1e-06, F32))
-    for p in range(EARLY, PIECES):
-        mix(p)
+    mix(ORDER[4])
     for r in range(4):
         remote(FWD + r, block(2, r), block(2, r), at_x(1)).wait_recv()
-
-    @pl.loop(0, 2)
-    def _(w):
-        for k in range(N // TILE):
-            rows = pl.ds(k * TILE, TILE)
-            product = jnp.dot(mixed[w, rows, :], unit[...].reshape(N, N), preferred_element_type=F32)
-            half[rows] = (product * scale).astype(BF16)
-        for k in range(N // TILE):
-            rows = pl.ds(k * TILE, TILE)
-            side = unit[:, :, k * TILE : (k + 1) * TILE].reshape(N, TILE)
-            product = lax.dot_general(side, half[...], (((0,), (0,)), ((), ())), preferred_element_type=F32)
-            grown[w, rows] = (product * (scale * (1.0 / math.sqrt(N)))).astype(BF16)
-        pltpu.make_async_copy(grown.at[w], env_o.at[w, 0], store_sem.at[w]).start()
+    unit_store = pltpu.make_async_copy(unit, unit_o, store_sem.at[2 * PIECES])
+    unit_store.start()
+
+    stores = []
+    for p in ORDER:
+        rows = rows_of(p)
+        if p == ORDER[5]:
+            mix(p)
+        product = jnp.dot(mixed[:, rows, :].reshape(2 * PIECE, N), unit[...].reshape(N, N), preferred_element_type=F32)
+        half[:, rows] = (product * scale).astype(BF16).reshape(2, PIECE, N)
+        for w in range(2):
+            stores.append(pltpu.make_async_copy(half.at[w, rows], half_o.at[w, rows], store_sem.at[2 * p + w]))
+            stores[-1].start()
 
     for copy in (relay_up, relay_down, up_a, up_b, down_a, down_b):
         copy.wait_send()
@@ -309,31 +387,74 @@
         for copy in stage:
             copy.wait_send()
     for p in range(PIECES):
-        halo_up(p).wait_send()
-        halo_down(p).wait_send()
+        up_first(p, False).wait_send()
+        down_first(p, False).wait_send()
+    for p in range(HOPS):
+        pl.when(z == 0)(lambda: up_hop(p).wait_send())
+        pl.when(z == 3)(lambda: down_hop(p).wait_send())
+    for store in stores:
+        store.wait()
+    unit_store.wait()
+
+
+def last_product(matvec_h, half_h, unit_h, square_h, matvec_o, env_o, matvec, half, unit, square, grown, sem):
+    loads = [
+        pltpu.make_async_copy(unit_h, unit, sem.at[0]),
+        pltpu.make_async_copy(half_h.at[0], half.at[0], sem.at[1]),
+        pltpu.make_async_copy(half_h.at[1], half.at[1], sem.at[2]),
+        pltpu.make_async_copy(square_h, square, sem.at[3]),
+        pltpu.make_async_copy(matvec_h, matvec, sem.at[4]),
+    ]
+    for load in loads:
+        load.start()
+    loads[3].wait()
+    factor = lax.rsqrt(jnp.full((1, N), jnp.sum(square[...]) * (1.0 / (8 * N * N)) + 1e-06, F32)) * (1.0 / math.sqrt(N))
+    loads[4].wait()
+    stores = [pltpu.make_async_copy(matvec, matvec_o, sem.at[5])]
+    stores[0].start()
+    loads[0].wait()
     for w in range(2):
-        pltpu.make_async_copy(grown.at[w], env_o.at[w, 0], store_sem.at[w]).wait()
+        loads[1 + w].wait()
+        for k in range(N // TILE):
+            rows = pl.ds(k * TILE, TILE)
+            side = unit[:, :, k * TILE : (k + 1) * TILE].reshape(N, TILE)
+            product = lax.dot_general(side, half[w], (((0,), (0,)), ((), ())), preferred_element_type=F32)
+            grown[w, rows] = (product * factor).astype(BF16)
+            stores.append(pltpu.make_async_copy(grown.at[w, rows], env_o.at[w, 0, rows], sem.at[6 + 3 * w + k]))
+            stores[-1].start()
+    for store in stores:
+        store.wait()
 
 
 def on_device(
     theta, sector_dims, right_dims, env_left, env_right, mpo_on, mpo_coef, mix_index, weight_table
 ):
     hbm = pl.BlockSpec(memory_space=pl.ANY)
-    smem = pl.BlockSpec(memory_space=pltpu.SMEM)
-    matvec, env_next = pl.pallas_call(
+    vmem = pl.BlockSpec(memory_space=pltpu.VMEM)
+    matvec, half, unit, square = pl.pallas_call(
         body,
         out_shape=(
             jax.ShapeDtypeStruct((BLK, N), BF16),
-            jax.ShapeDtypeStruct(env_left.shape, BF16),
+            jax.ShapeDtypeStruct((2, N, N), BF16),
+            jax.ShapeDtypeStruct((16, BLK, N), BF16),
+            jax.ShapeDtypeStruct((8, 128), F32),
         ),
-        in_specs=[hbm, hbm, hbm, smem, smem, smem, smem, smem, smem],
-        out_specs=(pl.BlockSpec(memory_space=pltpu.VMEM), hbm),
+        in_specs=[hbm] * 9,
+        out_specs=(vmem, hbm, hbm, vmem),
         scratch_shapes=[
+            pltpu.SMEM((1,), jnp.int32),
+            pltpu.SMEM((1,), jnp.int32),
+            pltpu.SMEM((2,), jnp.int32),
+            pltpu.SMEM((2,), F32),
+            pltpu.SMEM((2, 3), jnp.int32),
+            pltpu.SMEM((8,), F32),
             pltpu.VMEM((N, N), BF16),
             pltpu.VMEM((2, N, N), BF16),
             pltpu.VMEM((2, N, N), BF16),
             pltpu.VMEM((N, N), BF16),
             pltpu.VMEM((N, N), BF16),
+            pltpu.VMEM((HOPS, PIECE, N), BF16),
+            pltpu.VMEM((HOPS, PIECE, N), BF16),
             pltpu.VMEM((4, 4, BLK, N), F32),
             pltpu.VMEM((2, 2, BLK, N), BF16),
             pltpu.VMEM((2, 2, BLK, N), BF16),
@@ -346,18 +467,34 @@
             pltpu.VMEM((5, 8, 128), F32),
             pltpu.VMEM((10, 8, 128), F32),
             pltpu.VMEM((2, N, N), BF16),
-            pltpu.VMEM((N, N), BF16),
             pltpu.VMEM((2, N, N), BF16),
+            pltpu.SemaphoreType.DMA((6,)),
             pltpu.SemaphoreType.DMA((5,)),
             pltpu.SemaphoreType.DMA((COPIES,)),
             pltpu.SemaphoreType.DMA((COPIES,)),
-            pltpu.SemaphoreType.DMA((2,)),
+            pltpu.SemaphoreType.DMA((2 * PIECES + 1,)),
         ],
         compiler_params=pltpu.CompilerParams(
             collective_id=0, has_side_effects=True, vmem_limit_bytes=56 * 1024 * 1024
         ),
         name="sweep",
     )(theta, env_left, env_right, sector_dims, right_dims, mpo_on, mpo_coef, mix_index, weight_table)
+    matvec, env_next = pl.pallas_call(
+        last_product,
+        out_shape=(jax.ShapeDtypeStruct((BLK, N), BF16), jax.ShapeDtypeStruct(env_left.shape, BF16)),
+        in_specs=[hbm] * 4,
+        out_specs=(hbm, hbm),
+        scratch_shapes=[
+            pltpu.VMEM((BLK, N), BF16),
+            pltpu.VMEM((2, N, N), BF16),
+            pltpu.VMEM((16, BLK, N), BF16),
+            pltpu.VMEM((8, 128), F32),
+            pltpu.VMEM((2, N, N), BF16),
+            pltpu.SemaphoreType.DMA((12,)),
+        ],
+        compiler_params=pltpu.CompilerParams(vmem_limit_bytes=56 * 1024 * 1024),
+        name="last_product",
+    )(matvec, half, unit, square)
     return (matvec[None], env_next)
 
 

time: 77.3 us -> 69.1 us (0.89)
  local copies, waits for them, and re-layouts: 4.74 us -> 0 us
  Pallas kernels: 69.9 us -> 67 us
    pallas_call x1, Pallas kernels: 69.9 us -> 61.8 us  [on_device(): pl.pallas_call(body, out_shape=(jax.ShapeDtypeStruct((BLK, N), BF16), jax...]
    pallas_call x0 -> x1, Pallas kernels: none -> 5.25 us  [on_device(): pl.pallas_call(last_product, out_shape=(jax.ShapeDtypeStruct((BLK, N), BF...]
    unnamed x2 -> x0, local copies, waits for them, and re-layouts: 4.74 us -> none
where the time goes in v2:
time: 69.1 us; the launch traced here: 69 us
  Pallas kernels  67 us (97%)
  between operations  1.93 us (3%)
    pallas_call x1, Pallas kernels, on_device(): pl.pallas_call(body, out_shape=(jax.ShapeDtypeStruct((BLK, N), BF16), jax...  61.8 us
    pallas_call x1, Pallas kernels, on_device(): pl.pallas_call(last_product, out_shape=(jax.ShapeDtypeStruct((BLK, N), BF...  5.25 us

profile of v2, /device:TPU:0, one launch (start us, length us, event | category | flops | bytes accessed | tf_op | source)
XLA Modules:
  0.0 69.0 jit_solution(14764889847791814655)
XLA Ops:
  1.9 61.8 %sweep.1 = (bf16[48,768]{1,0:T(8,128)(2,1)}, bf16[2,768,768]{2,1,0:T(8,128)(2,1)}, bf16[16,48,768]{2,1,0:T(8,128)(2,1)}, f32[8,128]{1,0:T(8,128)}) custom-call(bf16[1,768,768]{2,1,0:T(8,128)(2,1)} %theta_h.1, bf16[2,1,768,768]{3,2,1,0:T(8,128)(2,1)} %left_h.1, bf16[2,1,768,768]{3,2,1,0:T(8,128)(2,1)} %right_h.1, s32[1]{0:T(128)S(6)} %copy.11.rows_h, ...), custom_call_target="tpu_custom_call" | custom-call | tf_op jit(solution)/shard_map/sweep/pallas_call | solution.py:434
  63.7 5.2 %last_product.1 = (bf16[48,768]{1,0:T(8,128)(2,1)}, bf16[2,1,768,768]{3,2,1,0:T(8,128)(2,1)}) custom-call(bf16[48,768]{1,0:T(8,128)(2,1)} %get-tuple-element.8.matvec_h, bf16[2,768,768]{2,1,0:T(8,128)(2,1)} %get-tuple-element.9.half_h, bf16[16,48,768]{2,1,0:T(8,128)(2,1)} %get-tuple-element.10.unit_h, f32[8,128]{1,0:T(8,128)} %get-tuple-element.11.square_h), custom_call_target="tpu_custom_call" | custom-call | tf_op jit(solution)/shard_map/last_product/pallas_call | solution.py:482

commit v3 on v2

--- a/solution.py
+++ b/solution.py
@@ -21,6 +21,7 @@
 EARLY = 4
 HOPS = 3
 ORDER = (3, 0, 1, 4, 5, 2)
+LIFT = 1024.0
 PIECE = N // PIECES
 TILE = 256
 
@@ -32,21 +33,19 @@
 FWD = 20
 SUM_CORE = 24
 SUM_Y = 25
-SUM_X = 28
-SUM_Z = 31
-HALO_UP = 34
+HALO_UP = 28
 HALO_DOWN = HALO_UP + PIECES
 HOP_UP = HALO_DOWN + PIECES
-HOP_DOWN = HOP_UP + HOPS
-COPIES = HOP_DOWN + HOPS
+HOP_DOWN = HOP_UP + PIECES
+COPIES = HOP_DOWN + PIECES
 
 
 def body(
     theta_h, left_h, right_h, rows_h, cols_h, on_h, coef_h, index_h, table_h,
-    matvec_o, half_o, unit_o, square_o,
+    matvec_o, half_o, turned_o, square_o,
     rows_s, cols_s, on_s, coef_s, index_s, table_s,
     live, left, right, low, high, via_up, via_down, acc, relay_out, relay_in, side_out, from_left, from_right,
-    z_out, z_in, unit, part, part_in, mixed, half,
+    z_out, z_in, unit, turned, part, part_in, mixed, half,
     small_sem, load_sem, send_sem, recv_sem, store_sem,
 ):
     x = lax.axis_index("bond_0")
@@ -65,11 +64,7 @@
 
     other = {"sector_1": 1 - c}
     bond = x * 4 + z
-    above = lax.rem(bond + 1, 16)
-    below = lax.rem(bond + 15, 16)
-    up = {"bond_0": above // 4, "bond_1": lax.rem(above, 4)}
-    down = {"bond_0": below // 4, "bond_1": lax.rem(below, 4)}
-    peers = [at_x(1), at_x(2), at_x(3), at_z(1), at_z(2), at_z(3), at_y(1), at_y(2), at_y(3), other, up, down]
+    peers = [at_x(1), at_x(3), at_z(1), at_z(2), at_z(3), at_y(1), at_y(2), at_y(3), other]
 
     def remote(i, src, dst, device):
         return pltpu.make_async_remote_copy(
@@ -100,58 +95,67 @@
     def rows_of(p):
         return pl.ds(p * PIECE, PIECE)
 
-    def up_first(p, via):
-        target = via_up.at[p] if via else low.at[rows_of(p)]
-        return remote(HALO_UP + p, left_h.at[1, 0, rows_of(p)], target, at_z(1) if p < HOPS else up)
-
-    def down_first(p, via):
-        target = via_down.at[p] if via else high.at[rows_of(p)]
-        return remote(HALO_DOWN + p, left_h.at[0, 0, rows_of(p)], target, at_z(3) if p < HOPS else down)
-
-    def up_hop(p):
-        return remote(HOP_UP + p, via_up.at[p], low.at[rows_of(p)], at_x(1))
-
-    def down_hop(p):
-        return remote(HOP_DOWN + p, via_down.at[p], high.at[rows_of(p)], at_x(3))
-
-    def start_up(p):
-        if p < HOPS:
-            pl.when(z == 3)(lambda: up_first(p, True).start())
-            pl.when(z != 3)(lambda: up_first(p, False).start())
-        else:
-            up_first(p, False).start()
-
-    def start_down(p):
-        if p < HOPS:
-            pl.when(z == 0)(lambda: down_first(p, True).start())
-            pl.when(z != 0)(lambda: down_first(p, False).start())
-        else:
-            down_first(p, False).start()
+    class Side:
+        def __init__(self, channel, last, step, target, via, first, hop):
+            self.channel, self.last, self.step, self.target, self.via = channel, last, step, target, via
+            self.first_sem, self.hop_sem, self.receiver = first, hop, 3 - last
+
+        def source(self, p):
+            return left_h.at[self.channel, 0, rows_of(p)]
+
+        def along_z(self, p, source, target):
+            return remote(self.first_sem + p, source, target, at_z(self.step))
+
+        def along_x(self, p, source, target):
+            return remote(self.hop_sem + p, source, target, at_x(self.step))
+
+        def direct(self, p):
+            return self.along_z(p, self.source(p), self.target.at[rows_of(p)])
+
+        def leave(self, p):
+            if p < HOPS:
+                return self.along_z(p, self.source(p), self.via.at[p])
+            return self.along_x(p, self.source(p), self.via.at[p])
+
+        def onward(self, p):
+            if p < HOPS:
+                return self.along_x(p, self.via.at[p], self.target.at[rows_of(p)])
+            return self.along_z(p, self.via.at[p], self.target.at[rows_of(p)])
+
+        def start(self, p):
+            pl.when(z == self.last)(lambda: self.leave(p).start())
+            pl.when(z != self.last)(lambda: self.direct(p).start())
+
+        def relay(self, p):
+            @pl.when(z == (self.receiver if p < HOPS else self.last))
+            def _():
+                self.leave(p).wait_recv()
+                self.onward(p).start()
+
+        def arrive(self, p):
+            if p < HOPS:
+                pl.when(z == self.receiver)(lambda: self.onward(p).wait_recv())
+                pl.when(z != self.receiver)(lambda: self.direct(p).wait_recv())
+            else:
+                self.direct(p).wait_recv()
+
+        def sent(self, p):
+            self.direct(p).wait_send()
+            if p < HOPS:
+                pl.when(z == self.receiver)(lambda: self.onward(p).wait_send())
+            else:
+                pl.when(z == self.last)(lambda: self.leave(p).wait_send())
+
+    rising = Side(1, 3, 1, low, via_up, HALO_UP, HOP_UP)
+    falling = Side(0, 0, 3, high, via_down, HALO_DOWN, HOP_DOWN)
 
     def forward(p):
-        @pl.when(z == 0)
-        def _():
-            up_first(p, True).wait_recv()
-            up_hop(p).start()
-
-        @pl.when(z == 3)
-        def _():
-            down_first(p, True).wait_recv()
-            down_hop(p).start()
-
-    def halo_arrive(p):
-        if p < HOPS:
-            pl.when(z == 0)(lambda: up_hop(p).wait_recv())
-            pl.when(z != 0)(lambda: up_first(p, False).wait_recv())
-            pl.when(z == 3)(lambda: down_hop(p).wait_recv())
-            pl.when(z != 3)(lambda: down_first(p, False).wait_recv())
-        else:
-            up_first(p, False).wait_recv()
-            down_first(p, False).wait_recv()
+        rising.relay(p)
+        falling.relay(p)
 
     for p in range(EARLY):
-        start_up(p)
-        start_down(p)
+        rising.start(p)
+        falling.start(p)
 
     for load in smalls:
         load.wait()
@@ -221,18 +225,11 @@
     up_a.wait_recv()
     down_b.wait_recv()
 
-    @pl.when(z == 3)
-    def _():
-        for p in range(EARLY, PIECES):
-            start_up(p)
-
-    @pl.when(z == 0)
-    def _():
-        for p in range(EARLY, PIECES):
-            start_down(p)
-
-    forward(0)
-    forward(1)
+    for p in range(EARLY, PIECES):
+        pl.when(z == 3)(lambda: rising.leave(p).start())
+        pl.when(z == 0)(lambda: falling.leave(p).start())
+    for p in (0, 1, 3):
+        forward(p)
 
     def row_sum(j):
         return acc[2, j] + from_left[j].astype(F32) + from_right[j].astype(F32)
@@ -263,55 +260,14 @@
     ag_down[0].start()
 
     matvec_o[...] = rounded
-    square = mine * mine
-    tile = jnp.zeros((8, 128), F32)
-    for a in range(BLK // 8):
-        for b in range(N // 128):
-            tile = tile + square[a * 8 : a * 8 + 8, b * 128 : b * 128 + 128]
-    part[0] = tile
-
-    def spread(i, slot, devices):
-        return [
-            remote(i + n, part.at[slot], part_in.at[i - SUM_CORE + n], device) for n, device in enumerate(devices)
-        ]
-
-    sums = [
-        spread(SUM_CORE, 0, [other]),
-        spread(SUM_Y, 1, [at_y(1), at_y(2), at_y(3)]),
-        spread(SUM_X, 2, [at_x(1), at_x(2), at_x(3)]),
-        spread(SUM_Z, 3, [at_z(1), at_z(2), at_z(3)]),
-    ]
-    firsts = [0, 1, 4, 7]
-
-    def sum_start(stage):
-        for copy in sums[stage]:
-            copy.start()
-
-    def sum_finish(stage):
-        total = part[stage]
-        for n, copy in enumerate(sums[stage]):
-            copy.wait_recv()
-            total = total + part_in[firsts[stage] + n]
-        part[stage + 1] = total
-
-    sum_start(0)
     for d in (1, 3, 2):
         remote(AG_Z + d - 1, block(0, d), block(0, d), at_z(d)).wait_recv()
         ag_up[d].start()
         ag_down[d].start()
 
-    @pl.when(z != 3)
-    def _():
-        for p in range(EARLY, PIECES):
-            start_up(p)
-
-    @pl.when(z != 0)
-    def _():
-        for p in range(EARLY, PIECES):
-            start_down(p)
-
-    sum_finish(0)
-    sum_start(1)
+    for p in range(EARLY, PIECES):
+        pl.when(z != 3)(lambda: rising.direct(p).start())
+        pl.when(z != 0)(lambda: falling.direct(p).start())
 
     w_gain = [[table_s[index_s[w, k]] for k in range(3)] for w in range(2)]
     low_gain = jnp.where(bond > 0, w_gain[0][0], 0.0)
@@ -319,7 +275,8 @@
 
     def mix(p):
         rows = rows_of(p)
-        halo_arrive(p)
+        rising.arrive(p)
+        falling.arrive(p)
         here = left[0, rows].astype(F32)
         there = left[1, rows].astype(F32)
         mixed[0, rows] = (low_gain * low[rows].astype(F32) + w_gain[0][1] * here + w_gain[0][2] * there).astype(BF16)
@@ -334,45 +291,69 @@
         1: remote(FWD + 1, block(1, 1), block(1, 1), at_x(3)),
         2: remote(FWD + 2, block(1, 2), block(1, 2), at_x(3)),
     }
+    def squares(cx):
+        total = jnp.zeros((16, 128), F32)
+        for r in range(4):
+            value = block(cx, r)[...].astype(F32)
+            value = value * value
+            for a in range(BLK // 16):
+                for b in range(N // 128):
+                    total = total + value[a * 16 : a * 16 + 16, b * 128 : b * 128 + 128]
+        return total[:8] + total[8:]
+
     arrive(AG_UP, 3, 0)
     fwd[0].start()
     arrive(AG_DOWN, 1, 0)
     arrive(AG_DOWN, 1, 1)
     fwd[1].start()
+    forward(4)
     arrive(AG_UP, 3, 1)
-    sum_finish(1)
-    sum_start(2)
     arrive(AG_UP, 3, 3)
     fwd[3].start()
     arrive(AG_DOWN, 1, 3)
     arrive(AG_DOWN, 1, 2)
     fwd[2].start()
+    forward(5)
+    forward(2)
     arrive(AG_UP, 3, 2)
-    sum_finish(2)
-    sum_start(3)
-    forward(2)
-    for p in ORDER[:4]:
+    part[0] = squares(0) + squares(1) + squares(3)
+    for p in ORDER[:5]:
         mix(p)
-    sum_finish(3)
-    square_o[...] = part[4]
-    square_total = jnp.sum(part[4])
-    scale = lax.rsqrt(jnp.full((1, N), square_total * (1.0 / (8 * N * N)) + 1e-06, F32))
-    mix(ORDER[4])
     for r in range(4):
         remote(FWD + r, block(2, r), block(2, r), at_x(1)).wait_recv()
-    unit_store = pltpu.make_async_copy(unit, unit_o, store_sem.at[2 * PIECES])
-    unit_store.start()
+
+    part[0] = part[0] + squares(2)
+    sum_core = remote(SUM_CORE, part.at[0], part_in.at[0], other)
+    sum_y = [remote(SUM_Y + n, part.at[1], part_in.at[1 + n], at_y(1 + n)) for n in range(3)]
+    sum_core.start()
 
     stores = []
-    for p in ORDER:
+
+    def product(p):
         rows = rows_of(p)
-        if p == ORDER[5]:
-            mix(p)
-        product = jnp.dot(mixed[:, rows, :].reshape(2 * PIECE, N), unit[...].reshape(N, N), preferred_element_type=F32)
-        half[:, rows] = (product * scale).astype(BF16).reshape(2, PIECE, N)
+        result = jnp.dot(mixed[:, rows, :].reshape(2 * PIECE, N), unit[...].reshape(N, N), preferred_element_type=F32)
+        half[:, rows] = (result * LIFT).astype(BF16).reshape(2, PIECE, N)
         for w in range(2):
             stores.append(pltpu.make_async_copy(half.at[w, rows], half_o.at[w, rows], store_sem.at[2 * p + w]))
             stores[-1].start()
+
+    for p in ORDER[:3]:
+        product(p)
+    sum_core.wait_recv()
+    part[1] = part[0] + part_in[0]
+    for copy in sum_y:
+        copy.start()
+    for p in ORDER[3:5]:
+        product(p)
+    for k in range(N // TILE):
+        turned[k * TILE : (k + 1) * TILE] = unit[:, :, k * TILE : (k + 1) * TILE].reshape(N, TILE).T
+    turned_store = pltpu.make_async_copy(turned, turned_o, store_sem.at[2 * PIECES])
+    turned_store.start()
+    for copy in sum_y:
+        copy.wait_recv()
+    square_o[...] = part[1] + part_in[1] + part_in[2] + part_in[3]
+    mix(ORDER[5])
+    product(ORDER[5])
 
     for copy in (relay_up, relay_down, up_a, up_b, down_a, down_b):
         copy.wait_send()
@@ -383,23 +364,19 @@
         ag_up[r].wait_send()
         ag_down[r].wait_send()
         fwd[r].wait_send()
-    for stage in sums:
-        for copy in stage:
-            copy.wait_send()
+    for copy in [sum_core] + sum_y:
+        copy.wait_send()
     for p in range(PIECES):
-        up_first(p, False).wait_send()
-        down_first(p, False).wait_send()
-    for p in range(HOPS):
-        pl.when(z == 0)(lambda: up_hop(p).wait_send())
-        pl.when(z == 3)(lambda: down_hop(p).wait_send())
+        rising.sent(p)
+        falling.sent(p)
     for store in stores:
         store.wait()
-    unit_store.wait()
-
-
-def last_product(matvec_h, half_h, unit_h, square_h, matvec_o, env_o, matvec, half, unit, square, grown, sem):
+    turned_store.wait()
+
+
+def last_product(matvec_h, half_h, turned_h, square_h, matvec_o, env_o, matvec, half, turned, square, grown, sem):
     loads = [
-        pltpu.make_async_copy(unit_h, unit, sem.at[0]),
+        pltpu.make_async_copy(turned_h, turned, sem.at[0]),
         pltpu.make_async_copy(half_h.at[0], half.at[0], sem.at[1]),
         pltpu.make_async_copy(half_h.at[1], half.at[1], sem.at[2]),
         pltpu.make_async_copy(square_h, square, sem.at[3]),
@@ -408,7 +385,7 @@
     for load in loads:
         load.start()
     loads[3].wait()
-    factor = lax.rsqrt(jnp.full((1, N), jnp.sum(square[...]) * (1.0 / (8 * N * N)) + 1e-06, F32)) * (1.0 / math.sqrt(N))
+    scale = lax.rsqrt(jnp.full((1, N), jnp.sum(square[...]) * (1.0 / (8 * N * N)) + 1e-06, F32))
     loads[4].wait()
     stores = [pltpu.make_async_copy(matvec, matvec_o, sem.at[5])]
     stores[0].start()
@@ -417,9 +394,8 @@
         loads[1 + w].wait()
         for k in range(N // TILE):
             rows = pl.ds(k * TILE, TILE)
-            side = unit[:, :, k * TILE : (k + 1) * TILE].reshape(N, TILE)
-            product = lax.dot_general(side, half[w], (((0,), (0,)), ((), ())), preferred_element_type=F32)
-            grown[w, rows] = (product * factor).astype(BF16)
+            product = jnp.dot(turned[rows], half[w], preferred_element_type=F32)
+            grown[w, rows] = (product * scale * (scale * (1.0 / (LIFT * math.sqrt(N))))).astype(BF16)
             stores.append(pltpu.make_async_copy(grown.at[w, rows], env_o.at[w, 0, rows], sem.at[6 + 3 * w + k]))
             stores[-1].start()
     for store in stores:
@@ -431,12 +407,12 @@
 ):
     hbm = pl.BlockSpec(memory_space=pl.ANY)
     vmem = pl.BlockSpec(memory_space=pltpu.VMEM)
-    matvec, half, unit, square = pl.pallas_call(
+    matvec, half, turned, square = pl.pallas_call(
         body,
         out_shape=(
             jax.ShapeDtypeStruct((BLK, N), BF16),
             jax.ShapeDtypeStruct((2, N, N), BF16),
-            jax.ShapeDtypeStruct((16, BLK, N), BF16),
+            jax.ShapeDtypeStruct((N, N), BF16),
             jax.ShapeDtypeStruct((8, 128), F32),
         ),
         in_specs=[hbm] * 9,
@@ -453,8 +429,8 @@
             pltpu.VMEM((2, N, N), BF16),
             pltpu.VMEM((N, N), BF16),
             pltpu.VMEM((N, N), BF16),
-            pltpu.VMEM((HOPS, PIECE, N), BF16),
-            pltpu.VMEM((HOPS, PIECE, N), BF16),
+            pltpu.VMEM((PIECES, PIECE, N), BF16),
+            pltpu.VMEM((PIECES, PIECE, N), BF16),
             pltpu.VMEM((4, 4, BLK, N), F32),
             pltpu.VMEM((2, 2, BLK, N), BF16),
             pltpu.VMEM((2, 2, BLK, N), BF16),
@@ -464,8 +440,9 @@
             pltpu.VMEM((3, BLK, N), BF16),
             pltpu.VMEM((3, BLK, N), BF16),
             pltpu.VMEM((16, BLK, N), BF16),
-            pltpu.VMEM((5, 8, 128), F32),
-            pltpu.VMEM((10, 8, 128), F32),
+            pltpu.VMEM((N, N), BF16),
+            pltpu.VMEM((2, 8, 128), F32),
+            pltpu.VMEM((4, 8, 128), F32),
             pltpu.VMEM((2, N, N), BF16),
             pltpu.VMEM((2, N, N), BF16),
             pltpu.SemaphoreType.DMA((6,)),
@@ -487,14 +464,14 @@
         scratch_shapes=[
             pltpu.VMEM((BLK, N), BF16),
             pltpu.VMEM((2, N, N), BF16),
-            pltpu.VMEM((16, BLK, N), BF16),
+            pltpu.VMEM((N, N), BF16),
             pltpu.VMEM((8, 128), F32),
             pltpu.VMEM((2, N, N), BF16),
             pltpu.SemaphoreType.DMA((12,)),
         ],
         compiler_params=pltpu.CompilerParams(vmem_limit_bytes=56 * 1024 * 1024),
         name="last_product",
-    )(matvec, half, unit, square)
+    )(matvec, half, turned, square)
     return (matvec[None], env_next)
 
 

time: 69.1 us -> 63.5 us (0.919); the launches traced: 69 us -> 62.5 us
  Pallas kernels: 67 us -> 60.5 us
    pallas_call x1, Pallas kernels: 61.8 us -> 55.3 us  [on_device(): pl.pallas_call(body, out_shape=(jax.ShapeDtypeStruct((BLK, N), BF16), jax...]
where the time goes in v3:
time: 63.5 us; the launch traced here: 62.5 us
  Pallas kernels  60.5 us (95%)
  between operations  1.93 us (3%)
    pallas_call x1, Pallas kernels, on_device(): pl.pallas_call(body, out_shape=(jax.ShapeDtypeStruct((BLK, N), BF16), jax...  55.3 us
    pallas_call x1, Pallas kernels, on_device(): pl.pallas_call(last_product, out_shape=(jax.ShapeDtypeStruct((BLK, N), BF...  5.19 us

profile of v3, /device:TPU:0, one launch (start us, length us, event | category | flops | bytes accessed | tf_op | source)
XLA Modules:
  0.0 62.5 jit_solution(13108857192849417206)
XLA Ops:
  1.9 55.3 %sweep.1 = (bf16[48,768]{1,0:T(8,128)(2,1)}, bf16[2,768,768]{2,1,0:T(8,128)(2,1)}, bf16[768,768]{1,0:T(8,128)(2,1)}, f32[8,128]{1,0:T(8,128)}) custom-call(bf16[1,768,768]{2,1,0:T(8,128)(2,1)} %theta_h.1, bf16[2,1,768,768]{3,2,1,0:T(8,128)(2,1)} %left_h.1, bf16[2,1,768,768]{3,2,1,0:T(8,128)(2,1)} %right_h.1, s32[1]{0:T(128)S(6)} %copy.11.rows_h, ...), custom_call_target="tpu_custom_call" | custom-call | tf_op jit(solution)/shard_map/sweep/pallas_call | solution.py:410
  57.3 5.2 %last_product.1 = (bf16[48,768]{1,0:T(8,128)(2,1)}, bf16[2,1,768,768]{3,2,1,0:T(8,128)(2,1)}) custom-call(bf16[48,768]{1,0:T(8,128)(2,1)} %get-tuple-element.8.matvec_h, bf16[2,768,768]{2,1,0:T(8,128)(2,1)} %get-tuple-element.9.half_h, bf16[768,768]{1,0:T(8,128)(2,1)} %get-tuple-element.10.turned_h, f32[8,128]{1,0:T(8,128)} %get-tuple-element.11.square_h), custom_call_target="tpu_custom_call" | custom-call | tf_op jit(solution)/shard_map/last_product/pallas_call | solution.py:459

commit v4 on v3

v4 whole, which is shorter than its diff:
```python
import math

import jax
import jax.numpy as jnp
from jax import lax
from jax.experimental import pallas as pl
from jax.experimental.pallas import tpu as pltpu
from jax.sharding import Mesh
from jax.sharding import PartitionSpec as P

AXES = ("bond_0", "bond_1", "sector_0", "sector_1")
BOND = ("bond_0", "bond_1")
SECTOR = ("sector_0", "sector_1")
MESH = pl.DeviceIdType.MESH
F32 = jnp.float32
BF16 = jnp.bfloat16

N = 768
BLK = 48
SIZES = (96, 128, 128, 128, 144, 144)
PIECES = len(SIZES)
LAST = SIZES[-1]
SPLIT = 3
FIRST = (3, 4, 5, 0)
SECOND = (1, 2)
LIFT = 1024.0
TILE = 256

CHUNKS = 3
WIDTH = N // CHUNKS

RELAY_UP, RELAY_DOWN, UP_B, DOWN_A, UP_A, DOWN_B = range(0, 6 * CHUNKS, CHUNKS)
RS_Z = 6 * CHUNKS
AG_Z = 9 * CHUNKS
AG_UP, AG_DOWN, FWD_UP, FWD_DOWN = range(12 * CHUNKS, 16 * CHUNKS, CHUNKS)
SUM_Z = 16 * CHUNKS
SUM_X = SUM_Z + 3
SUM_S = SUM_X + 3
HALO_UP = SUM_S + 7
HALO_DOWN = HALO_UP + PIECES
HOP_UP = HALO_DOWN + PIECES
HOP_DOWN = HOP_UP + PIECES
COPIES = HOP_DOWN + PIECES


def body(
    theta_h, left_h, right_h, rows_h, cols_h, on_h, coef_h, index_h, table_h,
    matvec_o, half_o, turned_o, square_o,
    rows_s, cols_s, on_s, coef_s, index_s, table_s,
    live, left, right, low, high, via_up, via_down, acc, relay_out, relay_in, side_out, from_left, from_right,
    z_out, z_in, unit, turned, part, part_in, mixed, half,
    small_sem, load_sem, send_sem, recv_sem, store_sem,
):
    x = lax.axis_index("bond_0")
    z = lax.axis_index("bond_1")
    y = lax.axis_index("sector_0")
    c = lax.axis_index("sector_1")

    def at_x(d):
        return {"bond_0": lax.rem(x + d, 4)}

    def at_z(d):
        return {"bond_1": lax.rem(z + d, 4)}

    def at_y(d):
        return {"sector_0": lax.rem(y + d, 4)}

    other = {"sector_1": 1 - c}
    bond = x * 4 + z
    sectors = [other] + [at_y(d) for d in (1, 2, 3)] + [{**at_y(d), **other} for d in (1, 2, 3)]
    peers = [at_x(1), at_x(2), at_x(3), at_z(1), at_z(2), at_z(3)] + sectors

    def remote(i, src, dst, device):
        return pltpu.make_async_remote_copy(
            src_ref=src, dst_ref=dst, send_sem=send_sem.at[i], recv_sem=recv_sem.at[i],
            device_id=device, device_id_type=MESH,
        )

    loads = [
        pltpu.make_async_copy(theta_h.at[0], live, load_sem.at[0]),
        pltpu.make_async_copy(left_h.at[0, 0], left.at[0], load_sem.at[1]),
        pltpu.make_async_copy(left_h.at[1, 0], left.at[1], load_sem.at[2]),
        pltpu.make_async_copy(right_h.at[0, 0], right.at[0], load_sem.at[3]),
        pltpu.make_async_copy(right_h.at[1, 0], right.at[1], load_sem.at[4]),
    ]
    smalls = [
        pltpu.make_async_copy(source, target, small_sem.at[n])
        for n, (source, target) in enumerate(
            [(rows_h, rows_s), (cols_h, cols_s), (on_h, on_s), (coef_h, coef_s), (index_h, index_s), (table_h, table_s)]
        )
    ]
    barrier = pltpu.get_barrier_semaphore()
    for peer in peers:
        pl.semaphore_signal(barrier, inc=1, device_id=peer, device_id_type=MESH)
    for load in smalls + loads:
        load.start()
    pl.semaphore_wait(barrier, len(peers))

    def rows_of(p):
        return pl.ds(sum(SIZES[:p]), SIZES[p])

    class Side:
        def __init__(self, channel, last, step, target, via, first, hop):
            self.channel, self.last, self.step, self.target, self.via = channel, last, step, target, via
            self.first_sem, self.hop_sem, self.receiver = first, hop, 3 - last

        def stop(self, p):
            return self.via.at[p, pl.ds(0, SIZES[p])]

        def source(self, p):
            return left_h.at[self.channel, 0, rows_of(p)]

        def along_z(self, p, source, target):
            return remote(self.first_sem + p, source, target, at_z(self.step))

        def along_x(self, p, source, target):
            return remote(self.hop_sem + p, source, target, at_x(self.step))

        def direct(self, p):
            return self.along_z(p, self.source(p), self.target.at[rows_of(p)])

        def leave(self, p):
            if p >= SPLIT:
                return self.along_z(p, self.source(p), self.stop(p))
            return self.along_x(p, self.source(p), self.stop(p))

        def onward(self, p):
            if p >= SPLIT:
                return self.along_x(p, self.stop(p), self.target.at[rows_of(p)])
            return self.along_z(p, self.stop(p), self.target.at[rows_of(p)])

        def start(self, p):
            pl.when(z == self.last)(lambda: self.leave(p).start())
            pl.when(z != self.last)(lambda: self.direct(p).start())

        def relay(self, p):
            @pl.when(z == (self.receiver if p >= SPLIT else self.last))
            def _():
                self.leave(p).wait_recv()
                self.onward(p).start()

        def arrive(self, p):
            if p >= SPLIT:
                pl.when(z == self.receiver)(lambda: self.onward(p).wait_recv())
                pl.when(z != self.receiver)(lambda: self.direct(p).wait_recv())
            else:
                self.direct(p).wait_recv()

        def sent(self, p):
            self.direct(p).wait_send()
            if p >= SPLIT:
                pl.when(z == self.receiver)(lambda: self.onward(p).wait_send())
            else:
                pl.when(z == self.last)(lambda: self.leave(p).wait_send())

    rising = Side(1, 3, 1, low, via_up, HALO_UP, HOP_UP)
    falling = Side(0, 0, 3, high, via_down, HALO_DOWN, HOP_DOWN)

    def forward(p):
        rising.relay(p)
        falling.relay(p)

    for p in FIRST:
        rising.start(p)
        falling.start(p)

    for load in smalls:
        load.wait()
    row_dim = rows_s[0]
    col_dim = cols_s[0]
    loads[0].wait()

    @pl.loop(0, N // 128)
    def _(i):
        rows = pl.ds(pl.multiple_of(i * 128, 128), 128)
        row_id = lax.broadcasted_iota(jnp.int32, (128, N), 0) + i * 128
        col_id = lax.broadcasted_iota(jnp.int32, (128, N), 1)
        keep = (row_id < row_dim) & (col_id < col_dim)
        live[rows] = jnp.where(keep, live[rows].astype(F32), 0.0).astype(BF16)

    for load in loads[1:]:
        load.wait()

    gains = [coef_s[w] * on_s[w].astype(F32) for w in range(2)]

    chunks = range(CHUNKS)
    head, tail = pl.ds(0, 2), pl.ds(2, 2)
    relay_up = [remote(RELAY_UP + k, relay_out.at[0, k], relay_in.at[0, k], at_x(1)) for k in chunks]
    relay_down = [remote(RELAY_DOWN + k, relay_out.at[1, k], relay_in.at[1, k], at_x(3)) for k in chunks]
    up_b = [remote(UP_B + k, side_out.at[0, k, tail], from_left.at[k, tail], at_x(1)) for k in chunks]
    up_a = [remote(UP_A + k, side_out.at[0, k, head], from_left.at[k, head], at_x(1)) for k in chunks]
    down_a = [remote(DOWN_A + k, side_out.at[1, k, head], from_right.at[k, head], at_x(3)) for k in chunks]
    down_b = [remote(DOWN_B + k, side_out.at[1, k, tail], from_right.at[k, tail], at_x(3)) for k in chunks]

    def cols(k):
        return slice(k * WIDTH, (k + 1) * WIDTH)

    @pl.loop(0, 4)
    def _(i):
        owner = lax.rem(x + 2 + i, 4)
        rows = pl.ds(pl.multiple_of(owner * 192, 64), 192)
        total = None
        for w in range(2):
            applied = jnp.dot(left[w, rows, :], live[...], preferred_element_type=F32).astype(BF16)
            term = gains[w] * lax.dot_general(
                applied, right[w], (((1,), (1,)), ((), ())), preferred_element_type=F32
            )
            total = term if total is None else total + term
        acc[i] = total.reshape(4, BLK, N)

        @pl.when(i == 0)
        def _():
            for k in chunks:
                relay_out[0, k] = acc[0, 0:2, :, cols(k)].astype(BF16)
                relay_up[k].start()
                relay_out[1, k] = acc[0, 2:4, :, cols(k)].astype(BF16)
                relay_down[k].start()

        @pl.when(i == 1)
        def _():
            for k in chunks:
                side_out[1, k, 0:2] = acc[1, 0:2, :, cols(k)].astype(BF16)
                down_a[k].start()

        @pl.when(i == 3)
        def _():
            for k in chunks:
                side_out[0, k, 2:4] = acc[3, 2:4, :, cols(k)].astype(BF16)
                up_b[k].start()

    for k in chunks:
        relay_up[k].wait_recv()
        side_out[0, k, 0:2] = (acc[3, 0:2, :, cols(k)] + relay_in[0, k].astype(F32)).astype(BF16)
        up_a[k].start()
        relay_down[k].wait_recv()
        side_out[1, k, 2:4] = (acc[1, 2:4, :, cols(k)] + relay_in[1, k].astype(F32)).astype(BF16)
        down_b[k].start()

    def row_sum(k, j):
        return acc[2, j, :, cols(k)] + from_left[k, j].astype(F32) + from_right[k, j].astype(F32)

    def rs_z(k, d):
        return remote(RS_Z + 3 * k + d - 1, z_out.at[k, d - 1], z_in.at[k, d - 1], at_z(d))

    def sum_over_x(k):
        for copy in (up_b[k], down_a[k], up_a[k], down_b[k]):
            copy.wait_recv()
        for d in (2, 1, 3):
            z_out[k, d - 1] = row_sum(k, lax.rem(z + d, 4)).astype(BF16)
            rs_z(k, d).start()

    def own_block(k, d):
        return unit.at[k, x * 4 + lax.rem(z + 4 - d, 4)]

    def ag_z(k, d, shift):
        return remote(AG_Z + 3 * k + d - 1, own_block(k, shift), own_block(k, shift), at_z(d))

    def sum_over_z(k):
        mine = row_sum(k, z)
        for d in (1, 3, 2):
            rs_z(k, d).wait_recv()
            mine = mine + z_in[k, d - 1].astype(F32)
        row_id = lax.broadcasted_iota(jnp.int32, (BLK, WIDTH), 0) + bond * BLK
        col_id = lax.broadcasted_iota(jnp.int32, (BLK, WIDTH), 1) + k * WIDTH
        mine = jnp.where((row_id < row_dim) & (col_id < col_dim), mine, 0.0)
        rounded = mine.astype(BF16)
        unit[k, bond] = rounded
        matvec_o[:, cols(k)] = rounded
        for d in (2, 1, 3):
            ag_z(k, d, 0).start()
        square = mine * mine
        return sum(
            square[a : a + 8, b : b + 128] for a in range(0, BLK, 8) for b in range(0, WIDTH, 128)
        )

    def blocks(k, d, first, count):
        return unit.at[k, pl.ds(lax.rem(x + d, 4) * 4 + first, count)]

    def ag_up(k, d):
        return remote(AG_UP + k, blocks(k, d, 0, 4), blocks(k, d, 0, 4), at_x(1))

    def ag_down(k, d):
        return remote(AG_DOWN + k, blocks(k, d, 0, 4), blocks(k, d, 0, 4), at_x(3))

    def fwd_up(k, d):
        return remote(FWD_UP + k, blocks(k, d, 0, 2), blocks(k, d, 0, 2), at_x(1))

    def fwd_down(k, d):
        return remote(FWD_DOWN + k, blocks(k, d, 2, 2), blocks(k, d, 2, 2), at_x(3))

    def gather_z(k):
        for d in (1, 3, 2):
            ag_z(k, d, d).wait_recv()
        ag_up(k, 0).start()
        ag_down(k, 0).start()

    def gather_x(k):
        ag_up(k, 3).wait_recv()
        fwd_up(k, 3).start()
        ag_down(k, 1).wait_recv()
        fwd_down(k, 1).start()

    for k in chunks:
        sum_over_x(k)

    for p in SECOND:
        pl.when(z == 3)(lambda: rising.leave(p).start())
        pl.when(z == 0)(lambda: falling.leave(p).start())
    for p in (3, 4, 0):
        forward(p)

    def spread(i, stage, devices):
        return [
            remote(i + n, part.at[stage], part_in.at[i - SUM_Z + n], device) for n, device in enumerate(devices)
        ]

    sums = [
        spread(SUM_Z, 0, [at_z(1), at_z(2), at_z(3)]),
        spread(SUM_X, 1, [at_x(1), at_x(2), at_x(3)]),
        spread(SUM_S, 2, sectors),
    ]
    starts = [0, 3, 6, 13]

    def sum_start(stage, value):
        part[stage] = value
        for copy in sums[stage]:
            copy.start()

    def sum_finish(stage):
        for copy in sums[stage]:
            copy.wait_recv()
        return sum((part_in[n] for n in range(starts[stage], starts[stage + 1])), part[stage])

    sum_start(0, sum_over_z(0) + sum_over_z(1) + sum_over_z(2))
    for p in SECOND:
        pl.when(z != 3)(lambda: rising.direct(p).start())
        pl.when(z != 0)(lambda: falling.direct(p).start())

    forward(1)
    gather_z(0)
    gather_z(1)
    gather_z(2)
    sum_start(1, sum_finish(0))

    w_gain = [[table_s[index_s[w, k]] for k in range(3)] for w in range(2)]
    low_gain = jnp.where(bond > 0, w_gain[0][0], 0.0)
    high_gain = jnp.where(bond < 15, w_gain[1][2], 0.0)

    def mix(p):
        rows = rows_of(p)
        rising.arrive(p)
        falling.arrive(p)
        here = left[0, rows].astype(F32)
        there = left[1, rows].astype(F32)
        mixed[0, rows] = (low_gain * low[rows].astype(F32) + w_gain[0][1] * here + w_gain[0][2] * there).astype(BF16)
        mixed[1, rows] = (w_gain[1][0] * here + w_gain[1][1] * there + high_gain * high[rows].astype(F32)).astype(BF16)

    gather_x(0)
    gather_x(1)
    gather_x(2)
    forward(2)
    forward(5)
    sum_start(2, sum_finish(1))
    for p in (3, 0, 4, 1, 2):
        mix(p)

    stores = []

    def product(k, first, count, n):
        rows = pl.ds(first, count)
        for w in range(2):
            result = jnp.dot(mixed[w, rows, :], unit[k].reshape(N, WIDTH), preferred_element_type=F32)
            half[w, rows, cols(k)] = (result * LIFT).astype(BF16)
        area = half.at[:, rows, pl.ds(k * WIDTH, WIDTH)]
        stores.append(pltpu.make_async_copy(area, half_o.at[:, rows, pl.ds(k * WIDTH, WIDTH)], store_sem.at[n]))
        stores[-1].start()

    for k in chunks:
        fwd_up(k, 2).wait_recv()
        fwd_down(k, 2).wait_recv()
        product(k, 0, N - LAST, k)
        turned[cols(k)] = unit[k].reshape(N, WIDTH).T
        stores.append(pltpu.make_async_copy(turned.at[pl.ds(k * WIDTH, WIDTH)], turned_o.at[pl.ds(k * WIDTH, WIDTH)], store_sem.at[CHUNKS + k]))
        stores[-1].start()
    square_o[...] = sum_finish(2)
    mix(PIECES - 1)
    for k in chunks:
        product(k, N - LAST, LAST, 2 * CHUNKS + k)

    for k in chunks:
        for copy in (relay_up[k], relay_down[k], up_a[k], up_b[k], down_a[k], down_b[k]):
            copy.wait_send()
        for d in (1, 2, 3):
            rs_z(k, d).wait_send()
            ag_z(k, d, 0).wait_send()
        for copy in (ag_up(k, 0), ag_down(k, 0), fwd_up(k, 3), fwd_down(k, 1)):
            copy.wait_send()
    for stage in sums:
        for copy in stage:
            copy.wait_send()
    for p in range(PIECES):
        rising.sent(p)
        falling.sent(p)
    for store in stores:
        store.wait()


def last_product(matvec_h, half_h, turned_h, square_h, matvec_o, env_o, matvec, half, turned, square, grown, sem):
    loads = [
        pltpu.make_async_copy(turned_h, turned, sem.at[0]),
        pltpu.make_async_copy(half_h.at[0], half.at[0], sem.at[1]),
        pltpu.make_async_copy(half_h.at[1], half.at[1], sem.at[2]),
        pltpu.make_async_copy(square_h, square, sem.at[3]),
        pltpu.make_async_copy(matvec_h, matvec, sem.at[4]),
    ]
    for load in loads:
        load.start()
    loads[3].wait()
    scale = lax.rsqrt(jnp.full((1, N), jnp.sum(square[...]) * (1.0 / (8 * N * N)) + 1e-06, F32))
    loads[4].wait()
    stores = [pltpu.make_async_copy(matvec, matvec_o, sem.at[5])]
    stores[0].start()
    loads[0].wait()
    for w in range(2):
        loads[1 + w].wait()
        for k in range(N // TILE):
            rows = pl.ds(k * TILE, TILE)
            product = jnp.dot(turned[rows], half[w], preferred_element_type=F32)
            grown[w, rows] = (product * scale * (scale * (1.0 / (LIFT * math.sqrt(N))))).astype(BF16)
            stores.append(pltpu.make_async_copy(grown.at[w, rows], env_o.at[w, 0, rows], sem.at[6 + 3 * w + k]))
            stores[-1].start()
    for store in stores:
        store.wait()


def on_device(
    theta, sector_dims, right_dims, env_left, env_right, mpo_on, mpo_coef, mix_index, weight_table
):
    hbm = pl.BlockSpec(memory_space=pl.ANY)
    vmem = pl.BlockSpec(memory_space=pltpu.VMEM)
    matvec, half, turned, square = pl.pallas_call(
        body,
        out_shape=(
            jax.ShapeDtypeStruct((BLK, N), BF16),
            jax.ShapeDtypeStruct((2, N, N), BF16),
            jax.ShapeDtypeStruct((N, N), BF16),
            jax.ShapeDtypeStruct((8, 128), F32),
        ),
        in_specs=[hbm] * 9,
        out_specs=(vmem, hbm, hbm, vmem),
        scratch_shapes=[
            pltpu.SMEM((1,), jnp.int32),
            pltpu.SMEM((1,), jnp.int32),
            pltpu.SMEM((2,), jnp.int32),
            pltpu.SMEM((2,), F32),
            pltpu.SMEM((2, 3), jnp.int32),
            pltpu.SMEM((8,), F32),
            pltpu.VMEM((N, N), BF16),
            pltpu.VMEM((2, N, N), BF16),
            pltpu.VMEM((2, N, N), BF16),
            pltpu.VMEM((N, N), BF16),
            pltpu.VMEM((N, N), BF16),
            pltpu.VMEM((PIECES, max(SIZES), N), BF16),
            pltpu.VMEM((PIECES, max(SIZES), N), BF16),
            pltpu.VMEM((4, 4, BLK, N), F32),
            pltpu.VMEM((2, CHUNKS, 2, BLK, WIDTH), BF16),
            pltpu.VMEM((2, CHUNKS, 2, BLK, WIDTH), BF16),
            pltpu.VMEM((2, CHUNKS, 4, BLK, WIDTH), BF16),
            pltpu.VMEM((CHUNKS, 4, BLK, WIDTH), BF16),
            pltpu.VMEM((CHUNKS, 4, BLK, WIDTH), BF16),
            pltpu.VMEM((CHUNKS, 3, BLK, WIDTH), BF16),
            pltpu.VMEM((CHUNKS, 3, BLK, WIDTH), BF16),
            pltpu.VMEM((CHUNKS, 16, BLK, WIDTH), BF16),
            pltpu.VMEM((N, N), BF16),
            pltpu.VMEM((3, 8, 128), F32),
            pltpu.VMEM((13, 8, 128), F32),
            pltpu.VMEM((2, N, N), BF16),
            pltpu.VMEM((2, N, N), BF16),
            pltpu.SemaphoreType.DMA((6,)),
            pltpu.SemaphoreType.DMA((5,)),
            pltpu.SemaphoreType.DMA((COPIES,)),
            pltpu.SemaphoreType.DMA((COPIES,)),
            pltpu.SemaphoreType.DMA((3 * CHUNKS,)),
        ],
        compiler_params=pltpu.CompilerParams(
            collective_id=0, has_side_effects=True, vmem_limit_bytes=56 * 1024 * 1024
        ),
        name="sweep",
    )(theta, env_left, env_right, sector_dims, right_dims, mpo_on, mpo_coef, mix_index, weight_table)
    matvec, env_next = pl.pallas_call(
        last_product,
        out_shape=(jax.ShapeDtypeStruct((BLK, N), BF16), jax.ShapeDtypeStruct(env_left.shape, BF16)),
        in_specs=[hbm] * 4,
        out_specs=(hbm, hbm),
        scratch_shapes=[
            pltpu.VMEM((BLK, N), BF16),
            pltpu.VMEM((2, N, N), BF16),
            pltpu.VMEM((N, N), BF16),
            pltpu.VMEM((8, 128), F32),
            pltpu.VMEM((2, N, N), BF16),
            pltpu.SemaphoreType.DMA((12,)),
        ],
        compiler_params=pltpu.CompilerParams(vmem_limit_bytes=56 * 1024 * 1024),
        name="last_product",
    )(matvec, half, turned, square)
    return (matvec[None], env_next)


def solution(mesh):
    split = Mesh(mesh.devices.reshape(4, 4, 4, 2), AXES)
    in_specs = (
        P(SECTOR, None, None),
        P(SECTOR),
        P(SECTOR),
        P(BOND, SECTOR, None, None),
        P(BOND, SECTOR, None, None),
        P(BOND),
        P(BOND),
        P(BOND, None),
        P(),
    )
    out_specs = (P(SECTOR, BOND, None), P(BOND, SECTOR, None, None))
    return jax.shard_map(on_device, mesh=split, in_specs=in_specs, out_specs=out_specs, check_vma=False)
```

time: 63.5 us -> 59.5 us (0.937); the launches traced: 62.5 us -> 59.4 us
  Pallas kernels: 60.5 us -> 57.4 us
    pallas_call x1, Pallas kernels: 55.3 us -> 52.3 us  [on_device(): pl.pallas_call(body, out_shape=(jax.ShapeDtypeStruct((BLK, N), BF16), jax...]
where the time goes in v4:
time: 59.5 us; the launch traced here: 59.4 us
  Pallas kernels  57.4 us (96%)
  between operations  1.93 us (3%)
    pallas_call x1, Pallas kernels, on_device(): pl.pallas_call(body, out_shape=(jax.ShapeDtypeStruct((BLK, N), BF16), jax...  52.3 us
    pallas_call x1, Pallas kernels, on_device(): pl.pallas_call(last_product, out_shape=(jax.ShapeDtypeStruct((BLK, N), BF...  5.19 us

profile of v4, /device:TPU:0, one launch (start us, length us, event | category | flops | bytes accessed | tf_op | source)
XLA Modules:
  0.0 59.4 jit_solution(1407973256563026887)
XLA Ops:
  1.9 52.3 %sweep.1 = (bf16[48,768]{1,0:T(8,128)(2,1)}, bf16[2,768,768]{2,1,0:T(8,128)(2,1)}, bf16[768,768]{1,0:T(8,128)(2,1)}, f32[8,128]{1,0:T(8,128)}) custom-call(bf16[1,768,768]{2,1,0:T(8,128)(2,1)} %theta_h.1, bf16[2,1,768,768]{3,2,1,0:T(8,128)(2,1)} %left_h.1, bf16[2,1,768,768]{3,2,1,0:T(8,128)(2,1)} %right_h.1, s32[1]{0:T(128)S(6)} %copy.11.rows_h, ...), custom_call_target="tpu_custom_call" | custom-call | tf_op jit(solution)/shard_map/sweep/pallas_call | solution.py:441
  54.2 5.2 %last_product.1 = (bf16[48,768]{1,0:T(8,128)(2,1)}, bf16[2,1,768,768]{3,2,1,0:T(8,128)(2,1)}) custom-call(bf16[48,768]{1,0:T(8,128)(2,1)} %get-tuple-element.8.matvec_h, bf16[2,768,768]{2,1,0:T(8,128)(2,1)} %get-tuple-element.9.half_h, bf16[768,768]{1,0:T(8,128)(2,1)} %get-tuple-element.10.turned_h, f32[8,128]{1,0:T(8,128)} %get-tuple-element.11.square_h), custom_call_target="tpu_custom_call" | custom-call | tf_op jit(solution)/shard_map/last_product/pallas_call | solution.py:490

commit v5 on v4

--- a/solution.py
+++ b/solution.py
@@ -17,7 +17,7 @@
 
 N = 768
 BLK = 48
-SIZES = (96, 128, 128, 128, 144, 144)
+SIZES = (96, 128, 96, 160, 160, 128)
 PIECES = len(SIZES)
 LAST = SIZES[-1]
 SPLIT = 3
@@ -45,10 +45,10 @@
 
 def body(
     theta_h, left_h, right_h, rows_h, cols_h, on_h, coef_h, index_h, table_h,
-    matvec_o, half_o, turned_o, square_o,
+    matvec_o, env_o,
     rows_s, cols_s, on_s, coef_s, index_s, table_s,
     live, left, right, low, high, via_up, via_down, acc, relay_out, relay_in, side_out, from_left, from_right,
-    z_out, z_in, unit, turned, part, part_in, mixed, half,
+    z_out, z_in, unit, turned, part, part_in, mixed, half, grown_sum, grown,
     small_sem, load_sem, send_sem, recv_sem, store_sem,
 ):
     x = lax.axis_index("bond_0")
@@ -357,35 +357,45 @@
 
     gather_x(0)
     gather_x(1)
+    forward(2)
     gather_x(2)
-    forward(2)
     forward(5)
     sum_start(2, sum_finish(1))
     for p in (3, 0, 4, 1, 2):
         mix(p)
 
-    stores = []
-
-    def product(k, first, count, n):
+    def product(k, first, count):
         rows = pl.ds(first, count)
         for w in range(2):
             result = jnp.dot(mixed[w, rows, :], unit[k].reshape(N, WIDTH), preferred_element_type=F32)
             half[w, rows, cols(k)] = (result * LIFT).astype(BF16)
-        area = half.at[:, rows, pl.ds(k * WIDTH, WIDTH)]
-        stores.append(pltpu.make_async_copy(area, half_o.at[:, rows, pl.ds(k * WIDTH, WIDTH)], store_sem.at[n]))
-        stores[-1].start()
 
     for k in chunks:
         fwd_up(k, 2).wait_recv()
         fwd_down(k, 2).wait_recv()
-        product(k, 0, N - LAST, k)
+        product(k, 0, N - LAST)
         turned[cols(k)] = unit[k].reshape(N, WIDTH).T
-        stores.append(pltpu.make_async_copy(turned.at[pl.ds(k * WIDTH, WIDTH)], turned_o.at[pl.ds(k * WIDTH, WIDTH)], store_sem.at[CHUNKS + k]))
-        stores[-1].start()
-    square_o[...] = sum_finish(2)
+    for w in range(2):
+        for k in range(N // TILE):
+            rows = slice(k * TILE, (k + 1) * TILE)
+            grown_sum[w, rows] = jnp.dot(
+                turned[rows, : N - LAST], half[w, : N - LAST, :], preferred_element_type=F32
+            )
+    square_total = jnp.sum(sum_finish(2))
+    scale = lax.rsqrt(jnp.full((1, N), square_total * (1.0 / (8 * N * N)) + 1e-06, F32))
     mix(PIECES - 1)
     for k in chunks:
-        product(k, N - LAST, LAST, 2 * CHUNKS + k)
+        product(k, N - LAST, LAST)
+    stores = []
+    for w in range(2):
+        for k in range(N // TILE):
+            rows = pl.ds(k * TILE, TILE)
+            result = grown_sum[w, rows] + jnp.dot(
+                turned[rows, N - LAST :], half[w, N - LAST :, :], preferred_element_type=F32
+            )
+            grown[w, rows] = (result * scale * (scale * (1.0 / (LIFT * math.sqrt(N))))).astype(BF16)
+            stores.append(pltpu.make_async_copy(grown.at[w, rows], env_o.at[w, 0, rows], store_sem.at[3 * w + k]))
+            stores[-1].start()
 
     for k in chunks:
         for copy in (relay_up[k], relay_down[k], up_a[k], up_b[k], down_a[k], down_b[k]):
@@ -405,30 +415,20 @@
         store.wait()
 
 
-def last_product(matvec_h, half_h, turned_h, square_h, matvec_o, env_o, matvec, half, turned, square, grown, sem):
-    loads = [
-        pltpu.make_async_copy(turned_h, turned, sem.at[0]),
-        pltpu.make_async_copy(half_h.at[0], half.at[0], sem.at[1]),
-        pltpu.make_async_copy(half_h.at[1], half.at[1], sem.at[2]),
-        pltpu.make_async_copy(square_h, square, sem.at[3]),
-        pltpu.make_async_copy(matvec_h, matvec, sem.at[4]),
-    ]
+def hand_on(matvec_h, env_h, matvec_o, env_o, matvec, env, load_sem, store_sem):
+    loads = [pltpu.make_async_copy(matvec_h, matvec, load_sem.at[0])]
+    stores = [pltpu.make_async_copy(matvec, matvec_o, store_sem.at[0])]
+    for w in range(2):
+        for k in range(N // TILE):
+            n = 3 * w + k
+            rows = pl.ds(k * TILE, TILE)
+            loads.append(pltpu.make_async_copy(env_h.at[w, 0, rows], env.at[n], load_sem.at[n + 1]))
+            stores.append(pltpu.make_async_copy(env.at[n], env_o.at[w, 0, rows], store_sem.at[n + 1]))
     for load in loads:
         load.start()
-    loads[3].wait()
-    scale = lax.rsqrt(jnp.full((1, N), jnp.sum(square[...]) * (1.0 / (8 * N * N)) + 1e-06, F32))
-    loads[4].wait()
-    stores = [pltpu.make_async_copy(matvec, matvec_o, sem.at[5])]
-    stores[0].start()
-    loads[0].wait()
-    for w in range(2):
-        loads[1 + w].wait()
-        for k in range(N // TILE):
-            rows = pl.ds(k * TILE, TILE)
-            product = jnp.dot(turned[rows], half[w], preferred_element_type=F32)
-            grown[w, rows] = (product * scale * (scale * (1.0 / (LIFT * math.sqrt(N))))).astype(BF16)
-            stores.append(pltpu.make_async_copy(grown.at[w, rows], env_o.at[w, 0, rows], sem.at[6 + 3 * w + k]))
-            stores[-1].start()
+    for load, store in zip(loads, stores):
+        load.wait()
+        store.start()
     for store in stores:
         store.wait()
 
@@ -438,16 +438,14 @@
 ):
     hbm = pl.BlockSpec(memory_space=pl.ANY)
     vmem = pl.BlockSpec(memory_space=pltpu.VMEM)
-    matvec, half, turned, square = pl.pallas_call(
+    matvec, env_next = pl.pallas_call(
         body,
         out_shape=(
             jax.ShapeDtypeStruct((BLK, N), BF16),
-            jax.ShapeDtypeStruct((2, N, N), BF16),
-            jax.ShapeDtypeStruct((N, N), BF16),
-            jax.ShapeDtypeStruct((8, 128), F32),
+            jax.ShapeDtypeStruct(env_left.shape, BF16),
         ),
         in_specs=[hbm] * 9,
-        out_specs=(vmem, hbm, hbm, vmem),
+        out_specs=(vmem, hbm),
         scratch_shapes=[
             pltpu.SMEM((1,), jnp.int32),
             pltpu.SMEM((1,), jnp.int32),
@@ -476,11 +474,13 @@
             pltpu.VMEM((13, 8, 128), F32),
             pltpu.VMEM((2, N, N), BF16),
             pltpu.VMEM((2, N, N), BF16),
+            pltpu.VMEM((2, N, N), F32),
+            pltpu.VMEM((2, N, N), BF16),
             pltpu.SemaphoreType.DMA((6,)),
             pltpu.SemaphoreType.DMA((5,)),
             pltpu.SemaphoreType.DMA((COPIES,)),
             pltpu.SemaphoreType.DMA((COPIES,)),
-            pltpu.SemaphoreType.DMA((3 * CHUNKS,)),
+            pltpu.SemaphoreType.DMA((6,)),
         ],
         compiler_params=pltpu.CompilerParams(
             collective_id=0, has_side_effects=True, vmem_limit_bytes=56 * 1024 * 1024
@@ -488,21 +488,19 @@
         name="sweep",
     )(theta, env_left, env_right, sector_dims, right_dims, mpo_on, mpo_coef, mix_index, weight_table)
     matvec, env_next = pl.pallas_call(
-        last_product,
+        hand_on,
         out_shape=(jax.ShapeDtypeStruct((BLK, N), BF16), jax.ShapeDtypeStruct(env_left.shape, BF16)),
-        in_specs=[hbm] * 4,
+        in_specs=[hbm, hbm],
         out_specs=(hbm, hbm),
         scratch_shapes=[
             pltpu.VMEM((BLK, N), BF16),
-            pltpu.VMEM((2, N, N), BF16),
-            pltpu.VMEM((N, N), BF16),
-            pltpu.VMEM((8, 128), F32),
-            pltpu.VMEM((2, N, N), BF16),
-            pltpu.SemaphoreType.DMA((12,)),
+            pltpu.VMEM((6, TILE, N), BF16),
+            pltpu.SemaphoreType.DMA((7,)),
+            pltpu.SemaphoreType.DMA((7,)),
         ],
         compiler_params=pltpu.CompilerParams(vmem_limit_bytes=56 * 1024 * 1024),
-        name="last_product",
-    )(matvec, half, turned, square)
+        name="hand_on",
+    )(matvec, env_next)
     return (matvec[None], env_next)
 
 

time: 59.5 us -> 57.4 us (0.965)
  Pallas kernels: 57.4 us -> 55.4 us
    pallas_call x1, Pallas kernels: 5.19 us -> 2.55 us  [on_device(): pl.pallas_call(hand_on, out_shape=(jax.ShapeDtypeStruct((BLK, N), BF16),...]
where the time goes in v5:
time: 57.4 us; the launch traced here: 57.3 us
  Pallas kernels  55.4 us (97%)
  between operations  1.93 us (3%)
    pallas_call x1, Pallas kernels, on_device(): pl.pallas_call(body, out_shape=(jax.ShapeDtypeStruct((BLK, N), BF16), jax...  52.8 us
    pallas_call x1, Pallas kernels, on_device(): pl.pallas_call(hand_on, out_shape=(jax.ShapeDtypeStruct((BLK, N), BF16),...  2.55 us

profile of v5, /device:TPU:0, one launch (start us, length us, event | category | flops | bytes accessed | tf_op | source)
XLA Modules:
  0.0 57.3 jit_solution(18093567835590733924)
XLA Ops:
  1.9 52.8 %sweep.1 = (bf16[48,768]{1,0:T(8,128)(2,1)}, bf16[2,1,768,768]{3,2,1,0:T(8,128)(2,1)}) custom-call(bf16[1,768,768]{2,1,0:T(8,128)(2,1)} %theta_h.1, bf16[2,1,768,768]{3,2,1,0:T(8,128)(2,1)} %left_h.1, bf16[2,1,768,768]{3,2,1,0:T(8,128)(2,1)} %right_h.1, s32[1]{0:T(128)S(6)} %copy.11.rows_h, s32[1]{0:T(128)S(6)} %copy.12.cols_h, s32[2]{0:T(128)} %on_h.1, ...), custom_call_target="tpu_custom_call" | custom-call | tf_op jit(solution)/shard_map/sweep/pallas_call | solution.py:441
  54.7 2.6 %hand_on.1 = (bf16[48,768]{1,0:T(8,128)(2,1)}, bf16[2,1,768,768]{3,2,1,0:T(8,128)(2,1)}) custom-call(bf16[48,768]{1,0:T(8,128)(2,1)} %get-tuple-element.6.matvec_h, bf16[2,1,768,768]{3,2,1,0:T(8,128)(2,1)} %get-tuple-element.7.env_h), custom_call_target="tpu_custom_call" | custom-call | tf_op jit(solution)/shard_map/hand_on/pallas_call | solution.py:490

commit v6 on v5

--- a/solution.py
+++ b/solution.py
@@ -17,11 +17,11 @@
 
 N = 768
 BLK = 48
-SIZES = (96, 128, 96, 160, 160, 128)
+SIZES = (80, 112, 96, 176, 176, 128)
 PIECES = len(SIZES)
 LAST = SIZES[-1]
 SPLIT = 3
-FIRST = (3, 4, 5, 0)
+FIRST = (3, 4, 0)
 SECOND = (1, 2)
 LIFT = 1024.0
 TILE = 256
@@ -300,12 +300,12 @@
         ag_down(k, 1).wait_recv()
         fwd_down(k, 1).start()
 
-    for k in chunks:
-        sum_over_x(k)
-
     for p in SECOND:
         pl.when(z == 3)(lambda: rising.leave(p).start())
         pl.when(z == 0)(lambda: falling.leave(p).start())
+    for k in chunks:
+        sum_over_x(k)
+
     for p in (3, 4, 0):
         forward(p)
 
@@ -335,6 +335,8 @@
     for p in SECOND:
         pl.when(z != 3)(lambda: rising.direct(p).start())
         pl.when(z != 0)(lambda: falling.direct(p).start())
+    rising.start(PIECES - 1)
+    falling.start(PIECES - 1)
 
     forward(1)
     gather_z(0)
@@ -356,8 +358,8 @@
         mixed[1, rows] = (w_gain[1][0] * here + w_gain[1][1] * there + high_gain * high[rows].astype(F32)).astype(BF16)
 
     gather_x(0)
+    forward(2)
     gather_x(1)
-    forward(2)
     gather_x(2)
     forward(5)
     sum_start(2, sum_finish(1))

time: 57.4 us -> 57 us (level); the launches traced: 57.3 us -> 56 us
  Pallas kernels: 55.4 us -> 54.1 us
    pallas_call x1, Pallas kernels: 52.8 us -> 51.5 us  [on_device(): pl.pallas_call(body, out_shape=(jax.ShapeDtypeStruct((BLK, N), BF16), jax...]
where the time goes in v6:
time: 57 us; the launch traced here: 56 us
  Pallas kernels  54.1 us (95%)
  between operations  1.93 us (3%)
    pallas_call x1, Pallas kernels, on_device(): pl.pallas_call(body, out_shape=(jax.ShapeDtypeStruct((BLK, N), BF16), jax...  51.5 us
    pallas_call x1, Pallas kernels, on_device(): pl.pallas_call(hand_on, out_shape=(jax.ShapeDtypeStruct((BLK, N), BF16),...  2.55 us

profile of v6, /device:TPU:0, one launch (start us, length us, event | category | flops | bytes accessed | tf_op | source)
XLA Modules:
  0.0 56.0 jit_solution(14396150518172201224)
XLA Ops:
  1.9 51.5 %sweep.1 = (bf16[48,768]{1,0:T(8,128)(2,1)}, bf16[2,1,768,768]{3,2,1,0:T(8,128)(2,1)}) custom-call(bf16[1,768,768]{2,1,0:T(8,128)(2,1)} %theta_h.1, bf16[2,1,768,768]{3,2,1,0:T(8,128)(2,1)} %left_h.1, bf16[2,1,768,768]{3,2,1,0:T(8,128)(2,1)} %right_h.1, s32[1]{0:T(128)S(6)} %copy.11.rows_h, s32[1]{0:T(128)S(6)} %copy.12.cols_h, s32[2]{0:T(128)} %on_h.1, ...), custom_call_target="tpu_custom_call" | custom-call | tf_op jit(solution)/shard_map/sweep/pallas_call | solution.py:443
  53.5 2.6 %hand_on.1 = (bf16[48,768]{1,0:T(8,128)(2,1)}, bf16[2,1,768,768]{3,2,1,0:T(8,128)(2,1)}) custom-call(bf16[48,768]{1,0:T(8,128)(2,1)} %get-tuple-element.6.matvec_h, bf16[2,1,768,768]{3,2,1,0:T(8,128)(2,1)} %get-tuple-element.7.env_h), custom_call_target="tpu_custom_call" | custom-call | tf_op jit(solution)/shard_map/hand_on/pallas_call | solution.py:492
